TPU v7x, 32 devices: a whole 2x2x4 slice. The times are simulated.
32 devices in a mesh: section: 4 (over y, x), expert: 8 (over z, core).
Axes of the slice: x: 2, y: 2, z: 4, core: 2. Of those that a mesh axis runs over, the one named last changes fastest.
Arguments:
- saved_inputs: bfloat16 [4, 2, 96, 3072], P('section', None, 'expert'), may hold values from -6 to 6
- expert_ids: int32 [4, 2, 96, 2], P('section'), may hold values from 0 to 3, all different within a row; in each aligned block of 12 rows (0 to 11, 12 to 23, ..., all dimensions but the last counted through in order) at most 9 rows name the same one
- combine: bfloat16 [4, 2, 96, 2], P('section'), may hold values from 0.19921875 to 1
- top_grad: bfloat16 [2, 96, 3072], P(None, 'expert'), may hold values from -6 to 6
- w_gate: bfloat16 [4, 3072, 32768], P('section', None, 'expert'), may hold values from -0.109375 to 0.109375
- w_up: bfloat16 [4, 3072, 32768], P('section', None, 'expert'), may hold values from -0.109375 to 0.109375
- w_down: bfloat16 [4, 32768, 3072], P('section', 'expert'), may hold values from -0.0625 to 0.0625
Outputs:
- input_grads: bfloat16 [4, 2, 96, 3072], P('section', None, 'expert')
- combine_grads: float32 [4, 2, 96, 2], P('section', None, 'expert')
Inputs may be any that keep to these rules, and one draw needn't show every extreme that they name: `expert_ids`: each token names 2 different experts. Among the 12 tokens of one index of expert in one layer and micro-batch, no expert is named more than 9 times, and some expert reaches 9.
All inputs are finite; a program needn't handle non-finite values.
Results may differ from a plain program's by a relative error of at most 0.018.
Values may be sent and summed in bfloat16 or wider, within the bound.
No kernel may reach another device: no remote copies, remote signals or barrier semaphores. Data moves between devices by JAX's collectives and lax.ppermute only.
A program may use at most 192 MiB of HBM per device.

v0:
```python
import jax
import jax.numpy as jnp
from jax import lax
from jax.sharding import PartitionSpec as P

EXPERTS = 4
CAP = 9


def shifted(shard, axis, by):
    length = lax.axis_size(axis)
    pairs = [(i, i + by) for i in range(length) if 0 <= i + by < length]
    return lax.ppermute(shard, axis, pairs)


def silu_parts(values):
    sig = jax.nn.sigmoid(values)
    return (values * sig, sig * (1.0 + values * (1.0 - sig)))


def slot_tables(chosen, experts, capacity):
    onehot = (chosen[:, :, None] == jnp.arange(experts, dtype=jnp.int32)).astype(jnp.int32)
    before = jnp.cumsum(onehot, axis=1) - onehot
    position = jnp.sum(before * onehot, axis=2)
    same_slot = (
        position[:, None, None, :] == jnp.arange(capacity, dtype=jnp.int32)[None, None, :, None]
    ).astype(jnp.int32)
    return (jnp.transpose(onehot, (0, 2, 1))[:, :, None, :] * same_slot).astype(jnp.float32)


def expert_grads(got_inputs, got_grads, weights, gate_part, lift_part, down_part):
    senders, capacity, width = got_inputs.shape
    inputs = got_inputs.reshape(senders * capacity, width)
    grads = got_grads.reshape(senders * capacity, width)
    pre_gate = jnp.dot(inputs, gate_part, preferred_element_type=jnp.float32)
    pre_lift = jnp.dot(inputs, lift_part, preferred_element_type=jnp.float32)
    hidden_grad = jnp.einsum("rd,fd->rf", grads, down_part, preferred_element_type=jnp.float32)
    active, slope = silu_parts(pre_gate)
    slot_grads = jnp.sum(hidden_grad * active * pre_lift, axis=-1)
    scaled = weights.reshape(-1)[:, None] * hidden_grad
    gate_grad = (scaled * pre_lift * slope).astype(jnp.bfloat16)
    lift_grad = (scaled * active).astype(jnp.bfloat16)
    moved = jnp.einsum("rf,df->rd", gate_grad, gate_part, preferred_element_type=jnp.float32)
    moved = moved + jnp.einsum(
        "rf,df->rd", lift_grad, lift_part, preferred_element_type=jnp.float32
    )
    return (moved.reshape(senders, capacity, width), slot_grads.reshape(senders, capacity))


def per_device(saved_inputs, expert_ids, combine, top_grad, w_gate, w_up, w_down):
    devices = lax.axis_size("expert")
    sections = lax.axis_size("section")
    my_index = lax.axis_index("expert")
    my_section = lax.axis_index("section")
    gate_part = w_gate[0]
    lift_part = w_up[0]
    down_part = w_down[0]
    micro = saved_inputs.shape[1]
    tokens = saved_inputs.shape[2]
    width = saved_inputs.shape[3]
    choose = expert_ids.shape[3]
    experts = EXPERTS
    capacity = CAP
    group = devices // experts
    own_expert = my_index // group
    grads_out = jnp.zeros(saved_inputs.shape[1:], jnp.bfloat16)
    slots_out = jnp.zeros((micro, tokens, choose), jnp.float32)
    passed = jnp.zeros((tokens, width), jnp.bfloat16)
    for step in range(micro + sections - 1):
        index = step - (sections - 1 - my_section)
        valid = (index >= 0) & (index < micro)
        current = jnp.clip(index, 0, micro - 1)
        inputs_now = lax.dynamic_index_in_dim(saved_inputs[0], current, 0, keepdims=False)
        from_top = lax.dynamic_index_in_dim(top_grad, current, 0, keepdims=False)
        upper = jnp.where(my_section == sections - 1, from_top, passed)
        chosen = lax.dynamic_index_in_dim(expert_ids[0], current, 0, keepdims=False).reshape(
            devices, tokens * choose
        )
        weights_all = (
            lax.dynamic_index_in_dim(combine[0], current, 0, keepdims=False)
            .reshape(devices, tokens * choose)
            .astype(jnp.float32)
        )
        tables = slot_tables(chosen, experts, capacity)
        recv_table = lax.dynamic_index_in_dim(tables, own_expert, 1, keepdims=False)
        recv_weights = jnp.einsum(
            "jcr,jr->jc", recv_table, weights_all, precision=lax.Precision.HIGHEST
        )
        send_table = lax.dynamic_index_in_dim(tables, my_index, 0, keepdims=False)
        place = jnp.sum(send_table.reshape(experts, capacity, tokens, choose), axis=3)
        place_half = place.astype(jnp.bfloat16)
        sent_inputs = jnp.einsum(
            "ect,td->ecd", place_half, inputs_now, preferred_element_type=jnp.float32
        ).astype(jnp.bfloat16)
        sent_grads = jnp.einsum(
            "ect,td->ecd", place_half, upper, preferred_element_type=jnp.float32
        ).astype(jnp.bfloat16)
        sent_inputs = jnp.repeat(sent_inputs, group, axis=0)
        sent_grads = jnp.repeat(sent_grads, group, axis=0)
        got_inputs, got_grads = (
            lax.all_to_all(sent_inputs, "expert", split_axis=0, concat_axis=0, tiled=True),
            lax.all_to_all(sent_grads, "expert", split_axis=0, concat_axis=0, tiled=True),
        )

        def active_case(first, second):
            return expert_grads(first, second, recv_weights, gate_part, lift_part, down_part)

        def empty_case(first, second):
            return (
                jnp.zeros((devices, capacity, width), jnp.float32),
                jnp.zeros((devices, capacity), jnp.float32),
            )

        part_moved, part_slots = lax.cond(valid, active_case, empty_case, got_inputs, got_grads)
        moved_half = part_moved.astype(jnp.bfloat16)
        slots_half = part_slots.astype(jnp.bfloat16)
        back_moved, back_slots = (
            lax.all_to_all(moved_half, "expert", split_axis=0, concat_axis=0, tiled=True),
            lax.all_to_all(slots_half, "expert", split_axis=0, concat_axis=0, tiled=True),
        )
        back_moved = jnp.sum(
            back_moved.astype(jnp.float32).reshape(experts, group, capacity, width), axis=1
        )
        back_slots = jnp.sum(
            back_slots.astype(jnp.float32).reshape(experts, group, capacity), axis=1
        )
        moved = jnp.einsum("ect,ecd->td", place, back_moved, precision=lax.Precision.HIGHEST)
        slot_grad = jnp.einsum(
            "ecr,ec->r", send_table, back_slots, precision=lax.Precision.HIGHEST
        ).reshape(tokens, choose)
        result = (upper.astype(jnp.float32) + moved).astype(jnp.bfloat16)
        old_grad = lax.dynamic_index_in_dim(grads_out, current, 0, keepdims=False)
        grads_out = lax.dynamic_update_index_in_dim(
            grads_out, jnp.where(valid, result, old_grad), current, 0
        )
        old_slots = lax.dynamic_index_in_dim(slots_out, current, 0, keepdims=False)
        slots_out = lax.dynamic_update_index_in_dim(
            slots_out, jnp.where(valid, slot_grad, old_slots), current, 0
        )
        passed = shifted(result, "section", -1)
    return (grads_out[None], slots_out[None])


def solution(mesh):
    placed = (
        P("section", None, "expert", None),
        P("section", None, None, None),
        P("section", None, None, None),
        P(None, "expert", None),
        P("section", None, "expert"),
        P("section", None, "expert"),
        P("section", "expert", None),
    )
    return jax.shard_map(
        per_device,
        mesh=mesh,
        in_specs=placed,
        out_specs=(P("section", None, "expert", None), P("section", None, "expert", None)),
        check_vma=False,
    )
```

profile of v0, /device:TPU:0, one launch (start us, length us, event | category | flops | bytes accessed | tf_op | source)
XLA Modules:
  0.0 705.3 jit_solution(5870007492429476042)
XLA Ops:
  6.3 6.5 all-to-all-start
  17.1 16.6 %all-to-all-done = bf16[8,9,3072]{2,1,0:T(8,128)(2,1)S(1)} async-done(((bf16[8,9,3072]{2,1,0:T(8,128)(2,1)}), bf16[8,9,3072]{2,1,0:T(8,128)(2,1)S(1)}, u32[]{:S(2)}, u32[]{:S(2)}) %all-to-all-start) | async-done | bytes 442400 | tf_op jit(solution)/shard_map/all_to_all | solution.py:102
  40.3 18.8 %all-to-all-done.1 = bf16[8,9,3072]{2,1,0:T(8,128)(2,1)S(1)} async-done(((bf16[8,9,3072]{2,1,0:T(8,128)(2,1)}), bf16[8,9,3072]{2,1,0:T(8,128)(2,1)S(1)}, u32[]{:S(2)}, u32[]{:S(2)}) %all-to-all-start.1) | async-done | bytes 442400 | tf_op jit(solution)/shard_map/all_to_all | solution.py:101
  68.7 19.0 %all-to-all-done.2 = bf16[8,9,3072]{2,1,0:T(8,128)(2,1)S(1)} async-done(((bf16[8,9,3072]{2,1,0:T(8,128)(2,1)}), bf16[8,9,3072]{2,1,0:T(8,128)(2,1)S(1)}, u32[]{:S(2)}, u32[]{:S(2)}) %all-to-all-start.2) | async-done | bytes 442400 | tf_op jit(solution)/shard_map/all_to_all | solution.py:118
  95.5 5.7 collective-permute-done
  101.4 11.7 %all-to-all-done.4 = bf16[8,9,3072]{2,1,0:T(8,128)(2,1)S(1)} async-done(((bf16[8,9,3072]{2,1,0:T(8,128)(2,1)}), bf16[8,9,3072]{2,1,0:T(8,128)(2,1)S(1)}, u32[]{:S(2)}, u32[]{:S(2)}) %all-to-all-start.4) | async-done | bytes 442400 | tf_op jit(solution)/shard_map/all_to_all | solution.py:101
  121.3 17.3 %all-to-all-done.3 = bf16[8,9,3072]{2,1,0:T(8,128)(2,1)S(1)} async-done(((bf16[8,9,3072]{2,1,0:T(8,128)(2,1)}), bf16[8,9,3072]{2,1,0:T(8,128)(2,1)S(1)}, u32[]{:S(2)}, u32[]{:S(2)}) %all-to-all-start.3) | async-done | bytes 442400 | tf_op jit(solution)/shard_map/all_to_all | solution.py:102
  147.3 20.0 %all-to-all-done.5 = bf16[8,9,3072]{2,1,0:T(8,128)(2,1)S(1)} async-done(((bf16[8,9,3072]{2,1,0:T(8,128)(2,1)}), bf16[8,9,3072]{2,1,0:T(8,128)(2,1)S(1)}, u32[]{:S(2)}, u32[]{:S(2)}) %all-to-all-start.5) | async-done | bytes 442400 | tf_op jit(solution)/shard_map/all_to_all | solution.py:118
  175.3 5.4 collective-permute-done.1
  181.0 11.7 %all-to-all-done.7 = bf16[8,9,3072]{2,1,0:T(8,128)(2,1)S(1)} async-done(((bf16[8,9,3072]{2,1,0:T(8,128)(2,1)}), bf16[8,9,3072]{2,1,0:T(8,128)(2,1)S(1)}, u32[]{:S(2)}, u32[]{:S(2)}) %all-to-all-start.7) | async-done | bytes 442400 | tf_op jit(solution)/shard_map/all_to_all | solution.py:101
  200.2 17.9 %all-to-all-done.6 = bf16[8,9,3072]{2,1,0:T(8,128)(2,1)S(1)} async-done(((bf16[8,9,3072]{2,1,0:T(8,128)(2,1)}), bf16[8,9,3072]{2,1,0:T(8,128)(2,1)S(1)}, u32[]{:S(2)}, u32[]{:S(2)}) %all-to-all-start.6) | async-done | bytes 442400 | tf_op jit(solution)/shard_map/all_to_all | solution.py:102
  228.4 18.4 %all-to-all-done.8 = bf16[8,9,3072]{2,1,0:T(8,128)(2,1)S(1)} async-done(((bf16[8,9,3072]{2,1,0:T(8,128)(2,1)}), bf16[8,9,3072]{2,1,0:T(8,128)(2,1)S(1)}, u32[]{:S(2)}, u32[]{:S(2)}) %all-to-all-start.8) | async-done | bytes 442400 | tf_op jit(solution)/shard_map/all_to_all | solution.py:118
  255.1 17.0 %all-to-all-done.10 = bf16[8,9,3072]{2,1,0:T(8,128)(2,1)S(1)} async-done(((bf16[8,9,3072]{2,1,0:T(8,128)(2,1)}), bf16[8,9,3072]{2,1,0:T(8,128)(2,1)S(1)}, u32[]{:S(2)}, u32[]{:S(2)}) %all-to-all-start.10) | async-done | bytes 442400 | tf_op jit(solution)/shard_map/all_to_all | solution.py:101
  275.4 141.4 %collective-permute-done.2 = bf16[12,3072]{1,0:T(8,128)(2,1)S(1)} collective-permute-done((bf16[12,3072]{1,0:T(8,128)(2,1)S(1)}, bf16[12,3072]{1,0:T(8,128)(2,1)S(1)}, u32[]{:S(2)}, u32[]{:S(2)}) %collective-permute-start.2) | collective-permute-done | bytes 73760 | tf_op jit(solution)/shard_map/ppermute | solution.py:13
  423.8 19.9 %all-to-all-done.9 = bf16[8,9,3072]{2,1,0:T(8,128)(2,1)S(1)} async-done(((bf16[8,9,3072]{2,1,0:T(8,128)(2,1)}), bf16[8,9,3072]{2,1,0:T(8,128)(2,1)S(1)}, u32[]{:S(2)}, u32[]{:S(2)}) %all-to-all-start.9) | async-done | bytes 442400 | tf_op jit(solution)/shard_map/all_to_all | solution.py:102
  447.0 63.7 %conditional.8 = (bf16[8,9,3072]{2,1,0:T(8,128)(2,1)}, bf16[8,9]{1,0:T(8,128)(2,1)}) conditional(s32[]{:T(128)} %convert_element_type.358, () %tuple.54, (f32[8,9]{1,0:T(8,128)S(1)}, bf16[8,9,3072]{2,1,0:T(8,128)(2,1)S(1)}, bf16[4096,3072]{1,0:T(8,128)(2,1)}, bf16[8,9,3072]{2,1,0:T(8,128)(2,1)S(1)}, bf16[3072,4096]{1,0:T(8,128)(2,1)}, ...), branch_computations={%region_24.25_spmd, %region_25.27_spmd} | conditional | flops 9067511808 | bytes 147359952 | solution.py:114
  447.4 10.6 %fusion.139 = f32[72,4096]{1,0:T(8,128)S(1)} fusion(bf16[72,3072]{1,0:T(8,128)(2,1)S(1)} %reshape.293, bf16[3072,4096]{1,0:T(8,128)(2,1)} %get-tuple-element.83), kind=kOutput, calls=%fused_computation.273 | convolution fusion | flops 1811939328 | bytes 26787840 | tf_op jit(solution)/shard_map/cond/branch_1_fun/dot_general | solution.py:35
  458.3 12.5 %fusion.138 = f32[72,4096]{1,0:T(8,128)S(1)} fusion(bf16[72,3072]{1,0:T(8,128)(2,1)S(1)} %reshape.292, bf16[4096,3072]{1,0:T(8,128)(2,1)} %get-tuple-element.80), kind=kOutput, calls=%fused_computation.272 | convolution fusion | flops 1811939328 | bytes 26787840 | tf_op jit(solution)/shard_map/cond/branch_1_fun/rd,fd->rf/dot_general | solution.py:37
  470.9 11.2 %multiply_reduce_fusion.3 = (bf16[72]{0:T(256)(128)(2,1)}, f32[72,4096]{1,0:T(8,128)S(1)}) fusion(f32[72,4096]{1,0:T(8,128)S(1)} %fusion.138, f32[72,4096]{1,0:T(8,128)S(1)} %fusion.139, bf16[72,3072]{1,0:T(8,128)(2,1)S(1)} %copy-done.7, bf16[3072,4096]{1,0:T(8,128)(2,1)} %get-tuple-element.82), kind=kOutput, calls=%fused_computation.37 | convolution fusion | flops 1814003584 | bytes 29147280 | tf_op jit(solution)/shard_map/cond/branch_1_fun/dot_general | solution.py:36
  482.1 13.5 %fusion.25 = f32[72,3072]{1,0:T(8,128)} fusion(bf16[3072,4096]{1,0:T(8,128)(2,1)} %get-tuple-element.83, f32[72,4096]{1,0:T(8,128)S(1)} %fusion.139, f32[72,4096]{1,0:T(8,128)S(1)} %get-tuple-element.133, f32[72,4096]{1,0:T(8,128)S(1)} %fusion.138, f32[72]{0:T(128)S(1)} %mul.208), kind=kOutput, calls=%fused_computation.42 | convolution fusion | flops 1815183360 | bytes 29589792 | tf_op jit(solution)/shard_map/cond/branch_1_fun/rf,df->rd/dot_general | solution.py:43
  495.7 13.0 %convolution_add_fusion.3 = bf16[72,3072]{1,0:T(8,128)(2,1)S(1)} fusion(f32[72,3072]{1,0:T(8,128)} %fusion.25, bf16[3072,4096]{1,0:T(8,128)(2,1)} %get-tuple-element.82, f32[72,4096]{1,0:T(8,128)S(1)} %fusion.138, f32[72]{0:T(128)S(1)} %mul.208, f32[72,4096]{1,0:T(8,128)S(1)} %fusion.139), kind=kOutput, calls=%fused_computation.36 | convolution fusion | flops 1814446080 | bytes 28852512 | tf_op jit(solution)/shard_map/cond/branch_1_fun/rf,df->rd/dot_general | solution.py:44
  510.7 5.1 all-to-all-start.11
  517.9 18.9 %all-to-all-done.11 = bf16[8,9,3072]{2,1,0:T(8,128)(2,1)S(1)} async-done(((bf16[8,9,3072]{2,1,0:T(8,128)(2,1)}), bf16[8,9,3072]{2,1,0:T(8,128)(2,1)S(1)}, u32[]{:S(2)}, u32[]{:S(2)}) %all-to-all-start.11) | async-done | bytes 442400 | tf_op jit(solution)/shard_map/all_to_all | solution.py:118
  544.6 17.6 %all-to-all-done.13 = bf16[8,9,3072]{2,1,0:T(8,128)(2,1)S(1)} async-done(((bf16[8,9,3072]{2,1,0:T(8,128)(2,1)}), bf16[8,9,3072]{2,1,0:T(8,128)(2,1)S(1)}, u32[]{:S(2)}, u32[]{:S(2)}) %all-to-all-start.13) | async-done | bytes 442400 | tf_op jit(solution)/shard_map/all_to_all | solution.py:101
  585.4 19.8 %all-to-all-done.12 = bf16[8,9,3072]{2,1,0:T(8,128)(2,1)S(1)} async-done(((bf16[8,9,3072]{2,1,0:T(8,128)(2,1)}), bf16[8,9,3072]{2,1,0:T(8,128)(2,1)S(1)}, u32[]{:S(2)}, u32[]{:S(2)}) %all-to-all-start.12) | async-done | bytes 442400 | tf_op jit(solution)/shard_map/all_to_all | solution.py:102
  605.2 63.5 %conditional.9 = (bf16[8,9,3072]{2,1,0:T(8,128)(2,1)}, bf16[8,9]{1,0:T(8,128)(2,1)S(1)}) conditional(s32[]{:T(128)} %convert_element_type.369, () %tuple.56, (f32[8,9]{1,0:T(8,128)S(1)}, bf16[8,9,3072]{2,1,0:T(8,128)(2,1)S(1)}, bf16[4096,3072]{1,0:T(8,128)(2,1)}, bf16[8,9,3072]{2,1,0:T(8,128)(2,1)S(1)}, bf16[3072,4096]{1,0:T(8,128)(2,1)}, ...), branch_computations={%region_31.32_spmd, %region_32.34_spmd} | conditional | flops 9067511808 | bytes 147359952 | solution.py:114
  605.7 10.6 %fusion.141 = f32[72,4096]{1,0:T(8,128)S(1)} fusion(bf16[72,3072]{1,0:T(8,128)(2,1)S(1)} %reshape.297, bf16[3072,4096]{1,0:T(8,128)(2,1)} %get-tuple-element.89), kind=kOutput, calls=%fused_computation.275 | convolution fusion | flops 1811939328 | bytes 26787840 | tf_op jit(solution)/shard_map/cond/branch_1_fun/dot_general | solution.py:35
  616.6 12.5 %fusion.140 = f32[72,4096]{1,0:T(8,128)S(1)} fusion(bf16[72,3072]{1,0:T(8,128)(2,1)S(1)} %reshape.296, bf16[4096,3072]{1,0:T(8,128)(2,1)} %get-tuple-element.86), kind=kOutput, calls=%fused_computation.274 | convolution fusion | flops 1811939328 | bytes 26787840 | tf_op jit(solution)/shard_map/cond/branch_1_fun/rd,fd->rf/dot_general | solution.py:37
  629.1 11.3 %multiply_reduce_fusion.4 = (bf16[72]{0:T(256)(128)(2,1)}, f32[72,4096]{1,0:T(8,128)S(1)}) fusion(f32[72,4096]{1,0:T(8,128)S(1)} %fusion.140, f32[72,4096]{1,0:T(8,128)S(1)} %fusion.141, bf16[72,3072]{1,0:T(8,128)(2,1)S(1)} %copy-done.9, bf16[3072,4096]{1,0:T(8,128)(2,1)} %get-tuple-element.88), kind=kOutput, calls=%fused_computation.49 | convolution fusion | flops 1814003584 | bytes 29147280 | tf_op jit(solution)/shard_map/cond/branch_1_fun/dot_general | solution.py:36
  640.5 13.5 %fusion.33 = f32[72,3072]{1,0:T(8,128)} fusion(bf16[3072,4096]{1,0:T(8,128)(2,1)} %get-tuple-element.89, f32[72,4096]{1,0:T(8,128)S(1)} %fusion.141, f32[72,4096]{1,0:T(8,128)S(1)} %get-tuple-element.135, f32[72,4096]{1,0:T(8,128)S(1)} %fusion.140, f32[72]{0:T(128)S(1)} %mul.219), kind=kOutput, calls=%fused_computation.54 | convolution fusion | flops 1815183360 | bytes 29589792 | tf_op jit(solution)/shard_map/cond/branch_1_fun/rf,df->rd/dot_general | solution.py:43
  654.0 13.1 %convolution_add_fusion.4 = bf16[72,3072]{1,0:T(8,128)(2,1)S(1)} fusion(f32[72,3072]{1,0:T(8,128)} %fusion.33, bf16[3072,4096]{1,0:T(8,128)(2,1)} %get-tuple-element.88, f32[72,4096]{1,0:T(8,128)S(1)} %fusion.140, f32[72]{0:T(128)S(1)} %mul.219, f32[72,4096]{1,0:T(8,128)S(1)} %fusion.141), kind=kOutput, calls=%fused_computation.48 | convolution fusion | flops 1814446080 | bytes 28852512 | tf_op jit(solution)/shard_map/cond/branch_1_fun/rf,df->rd/dot_general | solution.py:44
  682.3 20.3 %all-to-all-done.14 = bf16[8,9,3072]{2,1,0:T(8,128)(2,1)S(1)} async-done(((bf16[8,9,3072]{2,1,0:T(8,128)(2,1)}), bf16[8,9,3072]{2,1,0:T(8,128)(2,1)S(1)}, u32[]{:S(2)}, u32[]{:S(2)}) %all-to-all-start.14) | async-done | bytes 442400 | tf_op jit(solution)/shard_map/all_to_all | solution.py:118
  (348 shorter events, 152.9 us)
Async XLA Ops:
  6.3 27.4 %all-to-all-start = ((bf16[8,9,3072]{2,1,0:T(8,128)(2,1)}), bf16[8,9,3072]{2,1,0:T(8,128)(2,1)S(1)}, u32[]{:S(2)}, u32[]{:S(2)}) async-start(bf16[8,9,3072]{2,1,0:T(8,128)(2,1)} %bitcast.16), calls=%async_computation | async-start | bytes 1572864 | tf_op jit(solution)/shard_map/all_to_all | solution.py:102
  34.7 24.4 %all-to-all-start.1 = ((bf16[8,9,3072]{2,1,0:T(8,128)(2,1)}), bf16[8,9,3072]{2,1,0:T(8,128)(2,1)S(1)}, u32[]{:S(2)}, u32[]{:S(2)}) async-start(bf16[8,9,3072]{2,1,0:T(8,128)(2,1)} %bitcast.20), calls=%async_computation.1 | async-start | bytes 1572864 | tf_op jit(solution)/shard_map/all_to_all | solution.py:101
  63.2 24.6 %all-to-all-start.2 = ((bf16[8,9,3072]{2,1,0:T(8,128)(2,1)}), bf16[8,9,3072]{2,1,0:T(8,128)(2,1)S(1)}, u32[]{:S(2)}, u32[]{:S(2)}) async-start(bf16[8,9,3072]{2,1,0:T(8,128)(2,1)} %get-tuple-element.102), calls=%async_computation.2 | async-start | bytes 1572864 | tf_op jit(solution)/shard_map/all_to_all | solution.py:118
  67.9 50.2 %copy-start.32 = (f32[1,4,9,24]{2,3,1,0:T(8,128)}, f32[1,4,9,24]{2,3,1,0:T(8,128)S(1)}, u32[]{:S(2)}) copy-start(f32[1,4,9,24]{2,3,1,0:T(8,128)S(1)} %get-tuple-element.160) | copy-start | bytes 10372
  88.7 24.4 %all-to-all-start.4 = ((bf16[8,9,3072]{2,1,0:T(8,128)(2,1)}), bf16[8,9,3072]{2,1,0:T(8,128)(2,1)S(1)}, u32[]{:S(2)}, u32[]{:S(2)}) async-start(bf16[8,9,3072]{2,1,0:T(8,128)(2,1)} %bitcast.35), calls=%async_computation.4 | async-start | bytes 1572864 | tf_op jit(solution)/shard_map/all_to_all | solution.py:101
  94.2 7.0 collective-permute-start
  114.1 24.6 %all-to-all-start.3 = ((bf16[8,9,3072]{2,1,0:T(8,128)(2,1)}), bf16[8,9,3072]{2,1,0:T(8,128)(2,1)S(1)}, u32[]{:S(2)}, u32[]{:S(2)}) async-start(bf16[8,9,3072]{2,1,0:T(8,128)(2,1)} %bitcast.32), calls=%async_computation.3 | async-start | bytes 1572864 | tf_op jit(solution)/shard_map/all_to_all | solution.py:102
  142.7 25.6 %copy-start.70 = (bf16[8,9]{1,0:T(8,128)(2,1)}, bf16[8,9]{1,0:T(8,128)(2,1)S(1)}, u32[]{:S(2)}) copy-start(bf16[8,9]{1,0:T(8,128)(2,1)S(1)} %get-tuple-element.108) | copy-start | bytes 436
  142.7 24.6 %all-to-all-start.5 = ((bf16[8,9,3072]{2,1,0:T(8,128)(2,1)}), bf16[8,9,3072]{2,1,0:T(8,128)(2,1)S(1)}, u32[]{:S(2)}, u32[]{:S(2)}) async-start(bf16[8,9,3072]{2,1,0:T(8,128)(2,1)} %get-tuple-element.103), calls=%async_computation.5 | async-start | bytes 1572864 | tf_op jit(solution)/shard_map/all_to_all | solution.py:118
  168.2 24.4 %all-to-all-start.7 = ((bf16[8,9,3072]{2,1,0:T(8,128)(2,1)}), bf16[8,9,3072]{2,1,0:T(8,128)(2,1)S(1)}, u32[]{:S(2)}, u32[]{:S(2)}) async-start(bf16[8,9,3072]{2,1,0:T(8,128)(2,1)} %bitcast.49), calls=%async_computation.7 | async-start | bytes 1572864 | tf_op jit(solution)/shard_map/all_to_all | solution.py:101
  173.7 7.0 collective-permute-start.1
  193.6 24.4 %all-to-all-start.6 = ((bf16[8,9,3072]{2,1,0:T(8,128)(2,1)}), bf16[8,9,3072]{2,1,0:T(8,128)(2,1)S(1)}, u32[]{:S(2)}, u32[]{:S(2)}) async-start(bf16[8,9,3072]{2,1,0:T(8,128)(2,1)} %bitcast.46), calls=%async_computation.6 | async-start | bytes 1572864 | tf_op jit(solution)/shard_map/all_to_all | solution.py:102
  222.2 24.6 %all-to-all-start.8 = ((bf16[8,9,3072]{2,1,0:T(8,128)(2,1)}), bf16[8,9,3072]{2,1,0:T(8,128)(2,1)S(1)}, u32[]{:S(2)}, u32[]{:S(2)}) async-start(bf16[8,9,3072]{2,1,0:T(8,128)(2,1)} %get-tuple-element.104), calls=%async_computation.8 | async-start | bytes 1572864 | tf_op jit(solution)/shard_map/all_to_all | solution.py:118
  247.8 24.4 %all-to-all-start.10 = ((bf16[8,9,3072]{2,1,0:T(8,128)(2,1)}), bf16[8,9,3072]{2,1,0:T(8,128)(2,1)S(1)}, u32[]{:S(2)}, u32[]{:S(2)}) async-start(bf16[8,9,3072]{2,1,0:T(8,128)(2,1)} %bitcast.63), calls=%async_computation.10 | async-start | bytes 1572864 | tf_op jit(solution)/shard_map/all_to_all | solution.py:101
  251.4 165.4 %copy-start.24 = (bf16[1,12,3072]{2,0,1:T(2,128)(2,1)S(1)}, bf16[1,12,3072]{2,0,1:T(2,128)(2,1)}, u32[]{:S(2)}) copy-start(bf16[1,12,3072]{2,0,1:T(2,128)(2,1)} %get-tuple-element.142) | copy-start | bytes 221188
  253.2 164.8 %copy-start.16 = (bf16[2,12,3072]{2,1,0:T(8,128)(2,1)}, bf16[2,12,3072]{2,1,0:T(8,128)(2,1)S(1)}, u32[]{:S(2)}) copy-start(bf16[2,12,3072]{2,1,0:T(8,128)(2,1)S(1)} %get-tuple-element.122) | copy-start | bytes 442372
  253.2 163.5 %collective-permute-start.2 = (bf16[12,3072]{1,0:T(8,128)(2,1)S(1)}, bf16[12,3072]{1,0:T(8,128)(2,1)S(1)}, u32[]{:S(2)}, u32[]{:S(2)}) collective-permute-start(bf16[12,3072]{1,0:T(8,128)(2,1)S(1)} %get-tuple-element.123), channel_id=1, source_target_pairs={{8,0},{16,8},{24,16},{9,1},{17,9},{25,17},{10,2},{18,10},{26,18},{... | collective-permute-start | bytes 221192 | tf_op jit(solution)/shard_map/ppermute | solution.py:13
  272.2 144.9 %all-to-all-start.15 = ((bf16[8,1,9]{2,1,0:T(2,128)(2,1)}), bf16[8,1,9]{2,1,0:T(2,128)(2,1)S(1)}, u32[]{:S(2)}, u32[]{:S(2)}) async-start(bf16[8,1,9]{2,1,0:T(2,128)(2,1)} %copy.218), calls=%async_computation.15 | async-start | bytes 8192 | tf_op jit(solution)/shard_map/all_to_all | solution.py:119
  418.1 25.7 %all-to-all-start.9 = ((bf16[8,9,3072]{2,1,0:T(8,128)(2,1)}), bf16[8,9,3072]{2,1,0:T(8,128)(2,1)S(1)}, u32[]{:S(2)}, u32[]{:S(2)}) async-start(bf16[8,9,3072]{2,1,0:T(8,128)(2,1)} %bitcast.60), calls=%async_computation.9 | async-start | bytes 1572864 | tf_op jit(solution)/shard_map/all_to_all | solution.py:102
  443.7 67.0 %all-to-all-start.16 = ((bf16[8,1,9]{2,1,0:T(2,128)(2,1)}), bf16[8,1,9]{2,1,0:T(2,128)(2,1)S(1)}, u32[]{:S(2)}, u32[]{:S(2)}) async-start(bf16[8,1,9]{2,1,0:T(2,128)(2,1)} %copy.220), calls=%async_computation.16 | async-start | bytes 8192 | tf_op jit(solution)/shard_map/all_to_all | solution.py:119
  510.7 26.1 %all-to-all-start.11 = ((bf16[8,9,3072]{2,1,0:T(8,128)(2,1)}), bf16[8,9,3072]{2,1,0:T(8,128)(2,1)S(1)}, u32[]{:S(2)}, u32[]{:S(2)}) async-start(bf16[8,9,3072]{2,1,0:T(8,128)(2,1)} %get-tuple-element.105), calls=%async_computation.11 | async-start | bytes 1572864 | tf_op jit(solution)/shard_map/all_to_all | solution.py:118
  517.9 23.5 %copy-start.73 = (bf16[8,9]{1,0:T(8,128)(2,1)S(1)}, bf16[8,9]{1,0:T(8,128)(2,1)}, u32[]{:S(2)}) copy-start(bf16[8,9]{1,0:T(8,128)(2,1)} %copy-done.72) | copy-start | bytes 436
  517.9 24.1 %copy-start.17 = (bf16[2,12,3072]{2,1,0:T(8,128)(2,1)S(1)}, bf16[2,12,3072]{2,1,0:T(8,128)(2,1)}, u32[]{:S(2)}) copy-start(bf16[2,12,3072]{2,1,0:T(8,128)(2,1)} %copy-done.16) | copy-start | bytes 442372
  537.8 24.4 %all-to-all-start.13 = ((bf16[8,9,3072]{2,1,0:T(8,128)(2,1)}), bf16[8,9,3072]{2,1,0:T(8,128)(2,1)S(1)}, u32[]{:S(2)}, u32[]{:S(2)}) async-start(bf16[8,9,3072]{2,1,0:T(8,128)(2,1)} %bitcast.78), calls=%async_computation.13 | async-start | bytes 1572864 | tf_op jit(solution)/shard_map/all_to_all | solution.py:101
  542.0 32.9 %copy-start.22 = (bf16[1,12,3072]{2,0,1:T(2,128)(2,1)S(1)}, bf16[1,12,3072]{2,0,1:T(2,128)(2,1)}, u32[]{:S(2)}) copy-start(bf16[1,12,3072]{2,0,1:T(2,128)(2,1)} %get-tuple-element.141) | copy-start | bytes 221188
  543.3 37.5 %copy-start.18 = (bf16[2,12,3072]{2,1,0:T(8,128)(2,1)}, bf16[2,12,3072]{2,1,0:T(8,128)(2,1)S(1)}, u32[]{:S(2)}) copy-start(bf16[2,12,3072]{2,1,0:T(8,128)(2,1)S(1)} %get-tuple-element.120) | copy-start | bytes 442372
  543.3 31.0 %collective-permute-start.3 = (bf16[12,3072]{1,0:T(8,128)(2,1)S(1)}, bf16[12,3072]{1,0:T(8,128)(2,1)S(1)}, u32[]{:S(2)}, u32[]{:S(2)}) collective-permute-start(bf16[12,3072]{1,0:T(8,128)(2,1)S(1)} %get-tuple-element.121), channel_id=1, source_target_pairs={{8,0},{16,8},{24,16},{9,1},{17,9},{25,17},{10,2},{18,10},{26,18},{... | collective-permute-start | bytes 221192 | tf_op jit(solution)/shard_map/ppermute | solution.py:13
  562.2 8.7 %all-to-all-start.17 = ((bf16[8,1,9]{2,1,0:T(2,128)(2,1)}), bf16[8,1,9]{2,1,0:T(2,128)(2,1)S(1)}, u32[]{:S(2)}, u32[]{:S(2)}) async-start(bf16[8,1,9]{2,1,0:T(2,128)(2,1)} %copy.222), calls=%async_computation.17 | async-start | bytes 8192 | tf_op jit(solution)/shard_map/all_to_all | solution.py:119
  570.9 8.9 %all-to-all-start.18 = ((bf16[8,1,9]{2,1,0:T(2,128)(2,1)}), bf16[8,1,9]{2,1,0:T(2,128)(2,1)S(1)}, u32[]{:S(2)}, u32[]{:S(2)}) async-start(bf16[8,1,9]{2,1,0:T(2,128)(2,1)} %copy.224), calls=%async_computation.18 | async-start | bytes 8192 | tf_op jit(solution)/shard_map/all_to_all | solution.py:119
  580.8 24.4 %all-to-all-start.12 = ((bf16[8,9,3072]{2,1,0:T(8,128)(2,1)}), bf16[8,9,3072]{2,1,0:T(8,128)(2,1)S(1)}, u32[]{:S(2)}, u32[]{:S(2)}) async-start(bf16[8,9,3072]{2,1,0:T(8,128)(2,1)} %bitcast.75), calls=%async_computation.12 | async-start | bytes 1572864 | tf_op jit(solution)/shard_map/all_to_all | solution.py:102
  669.3 8.9 %all-to-all-start.19 = ((bf16[8,1,9]{2,1,0:T(2,128)(2,1)}), bf16[8,1,9]{2,1,0:T(2,128)(2,1)S(1)}, u32[]{:S(2)}, u32[]{:S(2)}) async-start(bf16[8,1,9]{2,1,0:T(2,128)(2,1)} %copy.226), calls=%async_computation.19 | async-start | bytes 8192 | tf_op jit(solution)/shard_map/all_to_all | solution.py:119
  678.2 24.4 %all-to-all-start.14 = ((bf16[8,9,3072]{2,1,0:T(8,128)(2,1)}), bf16[8,9,3072]{2,1,0:T(8,128)(2,1)S(1)}, u32[]{:S(2)}, u32[]{:S(2)}) async-start(bf16[8,9,3072]{2,1,0:T(8,128)(2,1)} %get-tuple-element.106), calls=%async_computation.14 | async-start | bytes 1572864 | tf_op jit(solution)/shard_map/all_to_all | solution.py:118
  (70 other events, 557.9 us)
where the time goes:
time: 711 us; the launch traced here: 705 us
  waiting for transfers between devices  431 us (61%)
  matrix products  132 us (19%)
  starting transfers between devices  81 us (11%)
  local copies, waits for them, and re-layouts  37.3 us (5%)
  loops' own time  10.6 us (1%)
  other arithmetic  10.1 us (1%)
    ppermute x4, waiting for transfers between devices, shifted(): return lax.ppermute(shard, axis, pairs)  153 us
    all_to_all x5, waiting for transfers between devices, per_device(): lax.all_to_all(moved_half, 'expert', split_axis=0, concat_axis=0, tiled=T...  96.6 us
    all_to_all x5, waiting for transfers between devices, per_device(): lax.all_to_all(sent_grads, 'expert', split_axis=0, concat_axis=0, tiled=T...  91.6 us
    all_to_all x5, waiting for transfers between devices, per_device(): lax.all_to_all(sent_inputs, 'expert', split_axis=0, concat_axis=0, tiled=...  76.9 us
    dot_general x2, matrix products, expert_grads(): jnp.einsum('rf,df->rd', gate_grad, gate_part, preferred_element_type=jnp....  27.1 us
    dot_general x2, matrix products, expert_grads(): jnp.einsum('rf,df->rd', lift_grad, lift_part, preferred_element_type=jnp....  26.1 us
    dot_general x2, matrix products, expert_grads(): jnp.einsum('rd,fd->rf', grads, down_part, preferred_element_type=jnp.floa...  25.1 us
    dot_general x2, matrix products, expert_grads(): pre_lift = jnp.dot(inputs, lift_part, preferred_element_type=jnp.float32)  22.5 us
  transfers between devices with their start and end apart: 24, of which 21 were waited for; matrix products, arithmetic and copies ran while one was open for 13% of the time, Pallas kernels for 0%

commit v1 on v0

v1 whole, which is shorter than its diff:
```python
import jax
import jax.numpy as jnp
from jax import lax
from jax.sharding import PartitionSpec as P

EXPERTS = 4


def silu_parts(values):
    sig = jax.nn.sigmoid(values)
    return (values * sig, sig * (1.0 + values * (1.0 - sig)))


def per_device(saved_inputs, expert_ids, combine, top_grad, w_gate, w_up, w_down):
    devices = lax.axis_size("expert")
    sections = lax.axis_size("section")
    lanes = devices // 2
    me = lax.axis_index("expert")
    my_section = lax.axis_index("section")
    my_lane, my_core = me // 2, me % 2
    own_expert = me // (devices // EXPERTS)
    gate_part, lift_part, down_part = w_gate[0], w_up[0], w_down[0]
    micro, tokens, width = saved_inputs.shape[1:]
    choose = expert_ids.shape[3]
    block = micro * tokens

    def to_core(rows):
        return lax.ppermute(rows, "expert", [(i, i ^ 1) for i in range(devices)])

    def to_lane(rows, k):
        return lax.ppermute(rows, "expert", [(i, i ^ (2 * k)) for i in range(devices)])

    def to_lower_lane(rows, k):
        pairs = [
            (s * devices + i, (s - 1) * devices + (i ^ (2 * k)))
            for s in range(1, sections)
            for i in range(devices)
        ]
        return lax.ppermute(rows, ("section", "expert"), pairs)

    def both_cores(mine):
        return jnp.concatenate([mine, to_core(mine)], axis=0)

    def gather(rows):
        return both_cores(
            jnp.concatenate([rows] + [to_lane(rows, k) for k in range(1, lanes)], axis=0)
        )

    lane_of = my_lane ^ jnp.arange(lanes)
    core_of = my_core ^ jnp.arange(2)
    source = (lane_of[None, :] * 2 + core_of[:, None]).reshape(-1)
    chosen = jnp.moveaxis(expert_ids[0].reshape(micro, devices, tokens, choose), 1, 0)
    weight = jnp.moveaxis(combine[0].reshape(micro, devices, tokens, choose), 1, 0)
    routed = jnp.sum(
        jnp.where(chosen == own_expert, weight.astype(jnp.float32), 0.0), axis=-1
    )
    routed = jnp.take(routed, source, axis=0).reshape(-1)

    inputs = gather(saved_inputs[0].reshape(block, width))
    upper = top_grad.reshape(block, width)
    upper_all = gather(upper)
    pre_gate = jnp.dot(inputs, gate_part, preferred_element_type=jnp.float32)
    pre_lift = jnp.dot(inputs, lift_part, preferred_element_type=jnp.float32)
    active, slope = silu_parts(pre_gate)
    to_gate = routed[:, None] * pre_lift * slope
    to_lift = routed[:, None] * active
    to_slot = active * pre_lift

    grads_out = jnp.zeros((block, width), jnp.bfloat16)
    slots_all = jnp.zeros((devices * block,), jnp.float32)
    for step in range(sections):
        valid = my_section == sections - 1 - step
        hidden = lax.dot_general(
            upper_all, down_part, (((1,), (1,)), ((), ())), preferred_element_type=jnp.float32
        )
        slots = jnp.sum(hidden * to_slot, axis=-1)
        slots_all = jnp.where(valid, slots, slots_all)
        gate_grad = (hidden * to_gate).astype(jnp.bfloat16)
        lift_grad = (hidden * to_lift).astype(jnp.bfloat16)
        moved = jnp.einsum("rf,df->rd", gate_grad, gate_part, preferred_element_type=jnp.float32)
        moved = moved + jnp.einsum(
            "rf,df->rd", lift_grad, lift_part, preferred_element_type=jnp.float32
        )
        half = lanes * block
        sent = moved[half:].astype(jnp.bfloat16)
        pair = (moved[:half] + to_core(sent).astype(jnp.float32)).reshape(lanes, block, width)
        total = upper.astype(jnp.float32) + pair[0]
        for k in range(1, lanes):
            total = total + to_lane(pair[k].astype(jnp.bfloat16), k).astype(jnp.float32)
        result = total.astype(jnp.bfloat16)
        grads_out = jnp.where(valid, result, grads_out)
        if step < sections - 1:
            arrived = [to_lower_lane(result, k) for k in range(lanes)]
            upper = arrived[0]
            upper_all = both_cores(jnp.concatenate(arrived, axis=0))

    half = lanes * block
    pair = slots_all[:half].astype(jnp.bfloat16).astype(jnp.float32) + to_core(
        slots_all[half:].astype(jnp.bfloat16)
    ).astype(jnp.float32)
    pair = pair.reshape(lanes, block)
    mine = [pair[0]] + [to_lane(pair[k], k) for k in range(1, lanes)]
    expert_of = (lane_of * 2) // (devices // EXPERTS)
    own_chosen = lax.dynamic_index_in_dim(chosen, me, 0, keepdims=False).reshape(block, choose)
    slots_out = jnp.zeros((block, choose), jnp.float32)
    for k in range(lanes):
        slots_out = slots_out + jnp.where(own_chosen == expert_of[k], mine[k][:, None], 0.0)
    return (
        grads_out.reshape(1, micro, tokens, width),
        slots_out.reshape(1, micro, tokens, choose),
    )


def solution(mesh):
    placed = (
        P("section", None, "expert", None),
        P("section", None, None, None),
        P("section", None, None, None),
        P(None, "expert", None),
        P("section", None, "expert"),
        P("section", None, "expert"),
        P("section", "expert", None),
    )
    return jax.shard_map(
        per_device,
        mesh=mesh,
        in_specs=placed,
        out_specs=(P("section", None, "expert", None), P("section", None, "expert", None)),
        check_vma=False,
    )
```

time: 711 us -> 441 us (0.62)
  waiting for transfers between devices: 431 us -> 112 us
  matrix products: 132 us -> 223 us
  starting transfers between devices: 81 us -> 48 us
  loops' own time: 10.6 us -> 0 us
    all_to_all x20 -> x0, waiting for transfers between devices: 279 us -> none  [the longest x5 96.6 us: per_device(): lax.all_to_all(moved_half, 'expert', split_axis=0, concat_axis=0, tiled=T...]
    dot_general x30 -> x14, matrix products: 132 us -> 223 us  [the longest x4 74.2 us: per_device(): jnp.einsum('rf,df->rd', lift_grad, lift_part, preferred_element_type=jnp....]
    all_to_all x20 -> x0, starting transfers between devices: 75.8 us -> none  [the longest x5 22 us: per_device(): lax.all_to_all(sent_grads, 'expert', split_axis=0, concat_axis=0, tiled=T...]
    ppermute x4 -> x43, starting transfers between devices: 5.17 us -> 48 us  [the longest x21 30 us: to_lane(): lax.ppermute(rows, 'expert', [(i, i ^ 2 * k) for i in range(devices)])]
    ppermute x4 -> x43, waiting for transfers between devices: 153 us -> 112 us  [the longest x21 63.2 us: to_lane(): lax.ppermute(rows, 'expert', [(i, i ^ 2 * k) for i in range(devices)])]
    unnamed x152 -> x39, local copies, waits for them, and re-layouts: 5.44 us -> 17.9 us
    another operation x5 -> x0, loops' own time: 10.6 us -> none  [per_device(): lax.cond(valid, active_case, empty_case, got_inputs, got_grads)]
    broadcast_in_dim x12 -> x3, local copies, waits for them, and re-layouts: 9.7 us -> 0.24 us  [per_device(): jnp.where(own_chosen == expert_of[k], mine[k][:, None], 0.0)]
  transfers between devices with their start and end apart: 24 -> 43, of which waited for: 21 -> 29; matrix products, arithmetic and copies ran while one was open for 13% -> 9% of each run, Pallas kernels for 0% -> 0%
where the time goes in v1:
time: 441 us; the launch traced here: 434 us
  matrix products  223 us (51%)
  waiting for transfers between devices  112 us (25%)
  starting transfers between devices  48 us (11%)
  local copies, waits for them, and re-layouts  32.6 us (7%)
  other arithmetic  17.1 us (4%)
    dot_general x4, matrix products, per_device(): jnp.einsum('rf,df->rd', lift_grad, lift_part, preferred_element_type=jnp....  74.2 us
    ppermute x21, waiting for transfers between devices, to_lane(): lax.ppermute(rows, 'expert', [(i, i ^ 2 * k) for i in range(devices)])  63.2 us
    dot_general x4, matrix products, per_device(): jnp.einsum('rf,df->rd', gate_grad, gate_part, preferred_element_type=jnp....  63.1 us
    dot_general x4, matrix products, per_device(): lax.dot_general(upper_all, down_part, (((1,), (1,)), ((), ())), preferred...  57.8 us
    ppermute x12, waiting for transfers between devices, to_lower_lane(): return lax.ppermute(rows, ('section', 'expert'), pairs)  43.1 us
    ppermute x21, starting transfers between devices, to_lane(): lax.ppermute(rows, 'expert', [(i, i ^ 2 * k) for i in range(devices)])  30 us
    unnamed x39, local copies, waits for them, and re-layouts  17.9 us
    ppermute x12, starting transfers between devices, to_lower_lane(): return lax.ppermute(rows, ('section', 'expert'), pairs)  15.5 us
  transfers between devices with their start and end apart: 43, of which 29 were waited for; matrix products, arithmetic and copies ran while one was open for 9% of the time, Pallas kernels for 0%

profile of v1, /device:TPU:0, one launch (start us, length us, event | category | flops | bytes accessed | tf_op | source)
XLA Modules:
  0.0 433.8 jit_solution(7631277955157800762)
XLA Ops:
  1.6 5.1 %collective-permute-start.6 = (bf16[24,3072]{1,0:T(8,128)(2,1)S(1)}, bf16[24,3072]{1,0:T(8,128)(2,1)S(1)}, u32[]{:S(2)}, u32[]{:S(2)}) collective-permute-start(bf16[24,3072]{1,0:T(8,128)(2,1)S(1)} %reshape_squeeze.8), channel_id=1, source_target_pairs={{0,6},{1,7},{2,4},{3,5},{4,2},{5,3},{6,0},{7,1},{8,14},{9,15},{10,... | collective-permute-start | bytes 442376 | tf_op jit(solution)/shard_map/ppermute | solution.py:31
  8.4 3.8 collective-permute-start.2
  18.4 8.1 %collective-permute-done.5 = bf16[24,3072]{1,0:T(8,128)(2,1)S(1)} collective-permute-done((bf16[24,3072]{1,0:T(8,128)(2,1)S(1)}, bf16[24,3072]{1,0:T(8,128)(2,1)S(1)}, u32[]{:S(2)}, u32[]{:S(2)}) %collective-permute-start.5) | collective-permute-done | bytes 147488 | tf_op jit(solution)/shard_map/ppermute | solution.py:31
  27.4 4.5 %collective-permute-done.1 = bf16[24,3072]{1,0:T(8,128)(2,1)S(1)} collective-permute-done((bf16[24,3072]{1,0:T(8,128)(2,1)S(1)}, bf16[24,3072]{1,0:T(8,128)(2,1)S(1)}, u32[]{:S(2)}, u32[]{:S(2)}) %collective-permute-start.1) | collective-permute-done | bytes 147488 | tf_op jit(solution)/shard_map/ppermute | solution.py:31
  36.9 13.4 %fusion.26 = f32[192,4096]{1,0:T(8,128)S(1)} fusion(bf16[192,3072]{1,0:T(8,128)(2,1)} %constant_dynamic-update-slice_fusion, bf16[1,4096,3072]{2,1,0:T(8,128)(2,1)} %param.13), kind=kOutput, calls=%fused_computation.27 | convolution fusion | flops 4831838208 | bytes 29491200 | tf_op jit(solution)/shard_map/dot_general | solution.py:73
  52.3 13.5 %fusion.8 = f32[192,4096]{1,0:T(8,128)S(1)} fusion(bf16[192,3072]{1,0:T(8,128)(2,1)} %constant_dynamic-update-slice_fusion.5, bf16[1,3072,4096]{2,1,0:T(8,128)(2,1)} %param.11), kind=kOutput, calls=%fused_computation.9 | convolution fusion | flops 4831838208 | bytes 29491200 | tf_op jit(solution)/shard_map/dot_general | solution.py:62
  65.8 14.1 %fusion.69 = (f32[192,4096]{1,0:T(8,128)}, f32[192,4096]{1,0:T(8,128)}) fusion(f32[192,4096]{1,0:T(8,128)S(1)} %fusion.8, f32[192]{0:T(256)S(1)} %select_n.153, bf16[192,3072]{1,0:T(8,128)(2,1)S(1)} %copy-done.5, bf16[1,3072,4096]{2,1,0:T(8,128)(2,1)} %param.12), kind=kOutput, calls=%fused_computation.136 | convolution fusion | flops 4840488960 | bytes 35783424 | tf_op jit(solution)/shard_map/dot_general | solution.py:63
  79.9 15.1 %fusion.6 = f32[192,3072]{1,0:T(8,128)} fusion(bf16[1,3072,4096]{2,1,0:T(8,128)(2,1)} %param.11, f32[192,4096]{1,0:T(8,128)S(1)} %fusion.26, f32[192,4096]{1,0:T(8,128)} %get-tuple-element.21), kind=kOutput, calls=%fused_computation.7 | convolution fusion | flops 4833411072 | bytes 33816576 | tf_op jit(solution)/shard_map/rf,df->rd/dot_general | solution.py:80
  95.0 26.0 %fusion.28 = f32[192,3072]{1,0:T(8,128)} fusion(f32[192,3072]{1,0:T(8,128)} %fusion.6, bf16[1,3072,4096]{2,1,0:T(8,128)(2,1)} %param.12, f32[192,4096]{1,0:T(8,128)S(1)} %fusion.26, f32[192]{0:T(256)S(1)} %select_n.153, f32[192,4096]{1,0:T(8,128)} %copy-done.7), kind=kOutput, calls=%fused_computation.29 | convolution fusion | flops 4837933056 | bytes 36176640 | tf_op jit(solution)/shard_map/rf,df->rd/dot_general | solution.py:81
  132.2 4.3 %collective-permute-done.11 = bf16[24,3072]{1,0:T(8,128)(2,1)S(1)} collective-permute-done((bf16[24,3072]{1,0:T(8,128)(2,1)S(1)}, bf16[24,3072]{1,0:T(8,128)(2,1)S(1)}, u32[]{:S(2)}, u32[]{:S(2)}) %collective-permute-start.11) | collective-permute-done | bytes 147488 | tf_op jit(solution)/shard_map/ppermute | solution.py:31
  136.5 6.3 %collective-permute-done.10 = bf16[24,3072]{1,0:T(8,128)(2,1)S(1)} collective-permute-done((bf16[24,3072]{1,0:T(8,128)(2,1)S(1)}, bf16[24,3072]{1,0:T(8,128)(2,1)S(1)}, u32[]{:S(2)}, u32[]{:S(2)}) %collective-permute-start.10) | collective-permute-done | bytes 147488 | tf_op jit(solution)/shard_map/ppermute | solution.py:31
  148.2 5.9 %collective-permute-done.15 = bf16[24,3072]{1,0:T(8,128)(2,1)S(1)} collective-permute-done((bf16[24,3072]{1,0:T(8,128)(2,1)S(1)}, bf16[24,3072]{1,0:T(8,128)(2,1)S(1)}, u32[]{:S(2)}, u32[]{:S(2)}) %collective-permute-start.15) | collective-permute-done | bytes 147488 | tf_op jit(solution)/shard_map/ppermute | solution.py:39
  154.1 5.4 %collective-permute-done.14 = bf16[24,3072]{1,0:T(8,128)(2,1)S(1)} collective-permute-done((bf16[24,3072]{1,0:T(8,128)(2,1)S(1)}, bf16[24,3072]{1,0:T(8,128)(2,1)S(1)}, u32[]{:S(2)}, u32[]{:S(2)}) %collective-permute-start.14) | collective-permute-done | bytes 147488 | tf_op jit(solution)/shard_map/ppermute | solution.py:39
  166.1 14.6 %fusion.24 = f32[192,4096]{1,0:T(8,128)} fusion(bf16[192,3072]{1,0:T(8,128)(2,1)} %constant_dynamic-update-slice_fusion.10, bf16[1,4096,3072]{2,1,0:T(8,128)(2,1)} %param.13), kind=kOutput, calls=%fused_computation.25 | convolution fusion | flops 4831838208 | bytes 29491200 | tf_op jit(solution)/shard_map/dot_general | solution.py:73
  180.7 16.0 %fusion.4 = f32[192,3072]{1,0:T(8,128)} fusion(bf16[1,3072,4096]{2,1,0:T(8,128)(2,1)} %param.11, f32[192,4096]{1,0:T(8,128)} %fusion.24, f32[192,4096]{1,0:T(8,128)} %get-tuple-element.21), kind=kOutput, calls=%fused_computation.5 | convolution fusion | flops 4833411072 | bytes 33816576 | tf_op jit(solution)/shard_map/rf,df->rd/dot_general | solution.py:80
  196.7 16.4 %fusion.31 = f32[192,3072]{1,0:T(8,128)} fusion(f32[192,3072]{1,0:T(8,128)} %fusion.4, bf16[1,3072,4096]{2,1,0:T(8,128)(2,1)} %param.12, f32[192,4096]{1,0:T(8,128)} %fusion.24, f32[192]{0:T(256)S(1)} %select_n.153, f32[192,4096]{1,0:T(8,128)} %copy-done.7), kind=kOutput, calls=%fused_computation.30 | convolution fusion | flops 4837933056 | bytes 36176640 | tf_op jit(solution)/shard_map/rf,df->rd/dot_general | solution.py:81
  224.3 3.9 collective-permute-done.20
  228.3 6.7 %collective-permute-done.19 = bf16[24,3072]{1,0:T(8,128)(2,1)S(1)} collective-permute-done((bf16[24,3072]{1,0:T(8,128)(2,1)S(1)}, bf16[24,3072]{1,0:T(8,128)(2,1)S(1)}, u32[]{:S(2)}, u32[]{:S(2)}) %collective-permute-start.19) | collective-permute-done | bytes 147488 | tf_op jit(solution)/shard_map/ppermute | solution.py:31
  240.3 6.5 %collective-permute-done.24 = bf16[24,3072]{1,0:T(8,128)(2,1)S(1)} collective-permute-done((bf16[24,3072]{1,0:T(8,128)(2,1)S(1)}, bf16[24,3072]{1,0:T(8,128)(2,1)S(1)}, u32[]{:S(2)}, u32[]{:S(2)}) %collective-permute-start.24) | collective-permute-done | bytes 147488 | tf_op jit(solution)/shard_map/ppermute | solution.py:39
  246.8 5.7 %collective-permute-done.23 = bf16[24,3072]{1,0:T(8,128)(2,1)S(1)} collective-permute-done((bf16[24,3072]{1,0:T(8,128)(2,1)S(1)}, bf16[24,3072]{1,0:T(8,128)(2,1)S(1)}, u32[]{:S(2)}, u32[]{:S(2)}) %collective-permute-start.23) | collective-permute-done | bytes 147488 | tf_op jit(solution)/shard_map/ppermute | solution.py:39
  258.4 14.9 %fusion.22 = f32[192,4096]{1,0:T(8,128)} fusion(bf16[192,3072]{1,0:T(8,128)(2,1)} %constant_dynamic-update-slice_fusion.15, bf16[1,4096,3072]{2,1,0:T(8,128)(2,1)} %param.13), kind=kOutput, calls=%fused_computation.23 | convolution fusion | flops 4831838208 | bytes 29491200 | tf_op jit(solution)/shard_map/dot_general | solution.py:73
  273.4 16.0 %fusion.2 = f32[192,3072]{1,0:T(8,128)} fusion(bf16[1,3072,4096]{2,1,0:T(8,128)(2,1)} %param.11, f32[192,4096]{1,0:T(8,128)} %fusion.22, f32[192,4096]{1,0:T(8,128)} %get-tuple-element.21), kind=kOutput, calls=%fused_computation.3 | convolution fusion | flops 4833411072 | bytes 33816576 | tf_op jit(solution)/shard_map/rf,df->rd/dot_general | solution.py:80
  289.3 16.4 %fusion.34 = f32[192,3072]{1,0:T(8,128)} fusion(f32[192,3072]{1,0:T(8,128)} %fusion.2, bf16[1,3072,4096]{2,1,0:T(8,128)(2,1)} %param.12, f32[192,4096]{1,0:T(8,128)} %fusion.22, f32[192]{0:T(256)S(1)} %select_n.153, f32[192,4096]{1,0:T(8,128)} %copy-done.7), kind=kOutput, calls=%fused_computation.31 | convolution fusion | flops 4837933056 | bytes 36176640 | tf_op jit(solution)/shard_map/rf,df->rd/dot_general | solution.py:81
  317.0 4.7 %collective-permute-done.29 = bf16[24,3072]{1,0:T(8,128)(2,1)S(1)} collective-permute-done((bf16[24,3072]{1,0:T(8,128)(2,1)S(1)}, bf16[24,3072]{1,0:T(8,128)(2,1)S(1)}, u32[]{:S(2)}, u32[]{:S(2)}) %collective-permute-start.29) | collective-permute-done | bytes 147488 | tf_op jit(solution)/shard_map/ppermute | solution.py:31
  321.6 6.0 %collective-permute-done.28 = bf16[24,3072]{1,0:T(8,128)(2,1)S(1)} collective-permute-done((bf16[24,3072]{1,0:T(8,128)(2,1)S(1)}, bf16[24,3072]{1,0:T(8,128)(2,1)S(1)}, u32[]{:S(2)}, u32[]{:S(2)}) %collective-permute-start.28) | collective-permute-done | bytes 147488 | tf_op jit(solution)/shard_map/ppermute | solution.py:31
  334.2 6.4 %collective-permute-done.33 = bf16[24,3072]{1,0:T(8,128)(2,1)S(1)} collective-permute-done((bf16[24,3072]{1,0:T(8,128)(2,1)}, bf16[24,3072]{1,0:T(8,128)(2,1)S(1)}, u32[]{:S(2)}, u32[]{:S(2)}) %collective-permute-start.33) | collective-permute-done | bytes 147488 | tf_op jit(solution)/shard_map/ppermute | solution.py:39
  340.6 6.3 %collective-permute-done.32 = bf16[24,3072]{1,0:T(8,128)(2,1)} collective-permute-done((bf16[24,3072]{1,0:T(8,128)(2,1)}, bf16[24,3072]{1,0:T(8,128)(2,1)}, u32[]{:S(2)}, u32[]{:S(2)}) %collective-permute-start.32) | collective-permute-done | bytes 147488 | tf_op jit(solution)/shard_map/ppermute | solution.py:39
  355.1 14.7 %fusion.20 = f32[192,4096]{1,0:T(8,128)} fusion(bf16[192,3072]{1,0:T(8,128)(2,1)} %constant_dynamic-update-slice_fusion.20, bf16[1,4096,3072]{2,1,0:T(8,128)(2,1)} %param.13), kind=kOutput, calls=%fused_computation.21 | convolution fusion | flops 4831838208 | bytes 29491200 | tf_op jit(solution)/shard_map/dot_general | solution.py:73
  369.8 16.0 %fusion = f32[192,3072]{1,0:T(8,128)} fusion(bf16[1,3072,4096]{2,1,0:T(8,128)(2,1)} %param.11, f32[192,4096]{1,0:T(8,128)} %fusion.20, f32[192,4096]{1,0:T(8,128)} %get-tuple-element.21), kind=kOutput, calls=%fused_computation.1 | convolution fusion | flops 4833411072 | bytes 33816576 | tf_op jit(solution)/shard_map/rf,df->rd/dot_general | solution.py:80
  385.8 5.7 %multiply_reduce_fusion = (bf16[192]{0:T(256)(128)(2,1)S(1)}, bf16[192]{0:T(256)(128)(2,1)S(1)}, bf16[192]{0:T(256)(128)(2,1)S(1)}, bf16[192]{0:T(256)(128)(2,1)S(1)}) fusion(f32[192,4096]{1,0:T(8,128)S(1)} %fusion.26, f32[192,4096]{1,0:T(8,128)} %get-tuple-element.20, f32[192,4096]{1,0:T(8,128)} %fusion.24, f32[192,4096]{1,0:T(8,128)} %fusion.22, ...), kind=kLoop, calls=%fused_computation.33 | loop fusion | flops 6290688 | bytes 15730176 | tf_op jit(solution)/shard_map/reduce_sum | solution.py:76
  391.5 15.4 %fusion.37 = f32[192,3072]{1,0:T(8,128)S(1)} fusion(f32[192,3072]{1,0:T(8,128)} %fusion, bf16[1,3072,4096]{2,1,0:T(8,128)(2,1)} %param.12, f32[192,4096]{1,0:T(8,128)} %fusion.20, f32[192]{0:T(256)S(1)} %select_n.153, f32[192,4096]{1,0:T(8,128)} %copy-done.7), kind=kOutput, calls=%fused_computation.32 | convolution fusion | flops 4837933056 | bytes 36176640 | tf_op jit(solution)/shard_map/rf,df->rd/dot_general | solution.py:81
  427.8 4.8 %collective-permute-done.37 = bf16[24,3072]{1,0:T(8,128)(2,1)S(1)} collective-permute-done((bf16[24,3072]{1,0:T(8,128)(2,1)S(1)}, bf16[24,3072]{1,0:T(8,128)(2,1)S(1)}, u32[]{:S(2)}, u32[]{:S(2)}) %collective-permute-start.37) | collective-permute-done | bytes 147488 | tf_op jit(solution)/shard_map/ppermute | solution.py:31
  (163 shorter events, 109.8 us)
Async XLA Ops:
  1.6 15.0 %collective-permute-start.6 = (bf16[24,3072]{1,0:T(8,128)(2,1)S(1)}, bf16[24,3072]{1,0:T(8,128)(2,1)S(1)}, u32[]{:S(2)}, u32[]{:S(2)}) collective-permute-start(bf16[24,3072]{1,0:T(8,128)(2,1)S(1)} %reshape_squeeze.8), channel_id=1, source_target_pairs={{0,6},{1,7},{2,4},{3,5},{4,2},{5,3},{6,0},{7,1},{8,14},{9,15},{10,... | collective-permute-start | bytes 442376 | tf_op jit(solution)/shard_map/ppermute | solution.py:31
  6.8 19.7 %collective-permute-start.5 = (bf16[24,3072]{1,0:T(8,128)(2,1)S(1)}, bf16[24,3072]{1,0:T(8,128)(2,1)S(1)}, u32[]{:S(2)}, u32[]{:S(2)}) collective-permute-start(bf16[24,3072]{1,0:T(8,128)(2,1)S(1)} %reshape_squeeze.8), channel_id=1, source_target_pairs={{0,4},{1,5},{2,6},{3,7},{4,0},{5,1},{6,2},{7,3},{8,12},{9,13},{10,... | collective-permute-start | bytes 442376 | tf_op jit(solution)/shard_map/ppermute | solution.py:31
  6.8 19.7 %collective-permute-start.4 = (bf16[24,3072]{1,0:T(8,128)(2,1)S(1)}, bf16[24,3072]{1,0:T(8,128)(2,1)S(1)}, u32[]{:S(2)}, u32[]{:S(2)}) collective-permute-start(bf16[24,3072]{1,0:T(8,128)(2,1)S(1)} %reshape_squeeze.8), channel_id=1, source_target_pairs={{0,2},{1,3},{2,0},{3,1},{4,6},{5,7},{6,4},{7,5},{8,10},{9,11},{10,... | collective-permute-start | bytes 442376 | tf_op jit(solution)/shard_map/ppermute | solution.py:31
  8.4 19.0 %collective-permute-start.2 = (bf16[24,3072]{1,0:T(8,128)(2,1)S(1)}, bf16[24,3072]{1,0:T(8,128)(2,1)S(1)}, u32[]{:S(2)}, u32[]{:S(2)}) collective-permute-start(bf16[24,3072]{1,0:T(8,128)(2,1)S(1)} %reshape.228), channel_id=1, source_target_pairs={{0,6},{1,7},{2,4},{3,5},{4,2},{5,3},{6,0},{7,1},{8,14},{9,15},{10,... | collective-permute-start | bytes 442376 | tf_op jit(solution)/shard_map/ppermute | solution.py:31
  12.2 19.7 %collective-permute-start.1 = (bf16[24,3072]{1,0:T(8,128)(2,1)S(1)}, bf16[24,3072]{1,0:T(8,128)(2,1)S(1)}, u32[]{:S(2)}, u32[]{:S(2)}) collective-permute-start(bf16[24,3072]{1,0:T(8,128)(2,1)S(1)} %reshape.228), channel_id=1, source_target_pairs={{0,4},{1,5},{2,6},{3,7},{4,0},{5,1},{6,2},{7,3},{8,12},{9,13},{10,... | collective-permute-start | bytes 442376 | tf_op jit(solution)/shard_map/ppermute | solution.py:31
  16.6 15.3 %collective-permute-start = (bf16[24,3072]{1,0:T(8,128)(2,1)S(1)}, bf16[24,3072]{1,0:T(8,128)(2,1)S(1)}, u32[]{:S(2)}, u32[]{:S(2)}) collective-permute-start(bf16[24,3072]{1,0:T(8,128)(2,1)S(1)} %reshape.228), channel_id=1, source_target_pairs={{0,2},{1,3},{2,0},{3,1},{4,6},{5,7},{6,4},{7,5},{8,10},{9,11},{10,... | collective-permute-start | bytes 442376 | tf_op jit(solution)/shard_map/ppermute | solution.py:31
  27.4 23.0 %collective-permute-start.7 = (bf16[96,3072]{1,0:T(8,128)(2,1)}, bf16[96,3072]{1,0:T(8,128)(2,1)}, u32[]{:S(2)}, u32[]{:S(2)}) collective-permute-start(bf16[96,3072]{1,0:T(8,128)(2,1)} %pad_maximum_fusion.1), channel_id=1, source_target_pairs={{0,1},{1,0},{2,3},{3,2},{4,5},{5,4},{6,7},{7,6},{8,9},{9,8},{10,11... | collective-permute-start | bytes 1769480 | tf_op jit(solution)/shard_map/ppermute | solution.py:28
  126.0 6.2 %collective-permute-start.9 = (bf16[24,3072]{1,0:T(8,128)(2,1)S(1)}, bf16[24,3072]{1,0:T(8,128)(2,1)S(1)}, u32[]{:S(2)}, u32[]{:S(2)}) collective-permute-start(bf16[24,3072]{1,0:T(8,128)(2,1)S(1)} %get-tuple-element.31), channel_id=1, source_target_pairs={{0,2},{1,3},{2,0},{3,1},{4,6},{5,7},{6,4},{7,5},{8,10},{9,11},{10,... | collective-permute-start | bytes 442376 | tf_op jit(solution)/shard_map/ppermute | solution.py:31
  126.1 10.5 %collective-permute-start.11 = (bf16[24,3072]{1,0:T(8,128)(2,1)S(1)}, bf16[24,3072]{1,0:T(8,128)(2,1)S(1)}, u32[]{:S(2)}, u32[]{:S(2)}) collective-permute-start(bf16[24,3072]{1,0:T(8,128)(2,1)S(1)} %get-tuple-element.32), channel_id=1, source_target_pairs={{0,6},{1,7},{2,4},{3,5},{4,2},{5,3},{6,0},{7,1},{8,14},{9,15},{10,... | collective-permute-start | bytes 442376 | tf_op jit(solution)/shard_map/ppermute | solution.py:31
  128.7 14.2 %collective-permute-start.10 = (bf16[24,3072]{1,0:T(8,128)(2,1)S(1)}, bf16[24,3072]{1,0:T(8,128)(2,1)S(1)}, u32[]{:S(2)}, u32[]{:S(2)}) collective-permute-start(bf16[24,3072]{1,0:T(8,128)(2,1)S(1)} %get-tuple-element.33), channel_id=1, source_target_pairs={{0,4},{1,5},{2,6},{3,7},{4,0},{5,1},{6,2},{7,3},{8,12},{9,13},{10,... | collective-permute-start | bytes 442376 | tf_op jit(solution)/shard_map/ppermute | solution.py:31
  143.0 11.1 %collective-permute-start.15 = (bf16[24,3072]{1,0:T(8,128)(2,1)S(1)}, bf16[24,3072]{1,0:T(8,128)(2,1)S(1)}, u32[]{:S(2)}, u32[]{:S(2)}) collective-permute-start(bf16[24,3072]{1,0:T(8,128)(2,1)S(1)} %fusion.60), channel_id=1, source_target_pairs={{8,6},{9,7},{10,4},{11,5},{12,2},{13,3},{14,0},{15,1},{16,14},{17,... | collective-permute-start | bytes 442376 | tf_op jit(solution)/shard_map/ppermute | solution.py:39
  144.3 15.2 %collective-permute-start.14 = (bf16[24,3072]{1,0:T(8,128)(2,1)S(1)}, bf16[24,3072]{1,0:T(8,128)(2,1)S(1)}, u32[]{:S(2)}, u32[]{:S(2)}) collective-permute-start(bf16[24,3072]{1,0:T(8,128)(2,1)S(1)} %fusion.60), channel_id=1, source_target_pairs={{8,4},{9,5},{10,6},{11,7},{12,0},{13,1},{14,2},{15,3},{16,12},{17,... | collective-permute-start | bytes 442376 | tf_op jit(solution)/shard_map/ppermute | solution.py:39
  145.6 13.9 %collective-permute-start.13 = (bf16[24,3072]{1,0:T(8,128)(2,1)S(1)}, bf16[24,3072]{1,0:T(8,128)(2,1)S(1)}, u32[]{:S(2)}, u32[]{:S(2)}) collective-permute-start(bf16[24,3072]{1,0:T(8,128)(2,1)S(1)} %fusion.60), channel_id=1, source_target_pairs={{8,2},{9,3},{10,0},{11,1},{12,6},{13,7},{14,4},{15,5},{16,10},{17,... | collective-permute-start | bytes 442376 | tf_op jit(solution)/shard_map/ppermute | solution.py:39
  146.9 15.6 %collective-permute-start.12 = (bf16[24,3072]{1,0:T(8,128)(2,1)S(1)}, bf16[24,3072]{1,0:T(8,128)(2,1)S(1)}, u32[]{:S(2)}, u32[]{:S(2)}) collective-permute-start(bf16[24,3072]{1,0:T(8,128)(2,1)S(1)} %fusion.60), channel_id=1, source_target_pairs={{8,0},{9,1},{10,2},{11,3},{12,4},{13,5},{14,6},{15,7},{16,8},{17,9... | collective-permute-start | bytes 442376 | tf_op jit(solution)/shard_map/ppermute | solution.py:39
  218.1 6.2 %collective-permute-start.18 = (bf16[24,3072]{1,0:T(8,128)(2,1)S(1)}, bf16[24,3072]{1,0:T(8,128)(2,1)S(1)}, u32[]{:S(2)}, u32[]{:S(2)}) collective-permute-start(bf16[24,3072]{1,0:T(8,128)(2,1)S(1)} %get-tuple-element.28), channel_id=1, source_target_pairs={{0,2},{1,3},{2,0},{3,1},{4,6},{5,7},{6,4},{7,5},{8,10},{9,11},{10,... | collective-permute-start | bytes 442376 | tf_op jit(solution)/shard_map/ppermute | solution.py:31
  218.9 9.4 %collective-permute-start.20 = (bf16[24,3072]{1,0:T(8,128)(2,1)S(1)}, bf16[24,3072]{1,0:T(8,128)(2,1)S(1)}, u32[]{:S(2)}, u32[]{:S(2)}) collective-permute-start(bf16[24,3072]{1,0:T(8,128)(2,1)S(1)} %get-tuple-element.29), channel_id=1, source_target_pairs={{0,6},{1,7},{2,4},{3,5},{4,2},{5,3},{6,0},{7,1},{8,14},{9,15},{10,... | collective-permute-start | bytes 442376 | tf_op jit(solution)/shard_map/ppermute | solution.py:31
  220.4 14.6 %collective-permute-start.19 = (bf16[24,3072]{1,0:T(8,128)(2,1)S(1)}, bf16[24,3072]{1,0:T(8,128)(2,1)S(1)}, u32[]{:S(2)}, u32[]{:S(2)}) collective-permute-start(bf16[24,3072]{1,0:T(8,128)(2,1)S(1)} %get-tuple-element.30), channel_id=1, source_target_pairs={{0,4},{1,5},{2,6},{3,7},{4,0},{5,1},{6,2},{7,3},{8,12},{9,13},{10,... | collective-permute-start | bytes 442376 | tf_op jit(solution)/shard_map/ppermute | solution.py:31
  235.1 11.7 %collective-permute-start.24 = (bf16[24,3072]{1,0:T(8,128)(2,1)S(1)}, bf16[24,3072]{1,0:T(8,128)(2,1)S(1)}, u32[]{:S(2)}, u32[]{:S(2)}) collective-permute-start(bf16[24,3072]{1,0:T(8,128)(2,1)S(1)} %fusion.56), channel_id=1, source_target_pairs={{8,6},{9,7},{10,4},{11,5},{12,2},{13,3},{14,0},{15,1},{16,14},{17,... | collective-permute-start | bytes 442376 | tf_op jit(solution)/shard_map/ppermute | solution.py:39
  236.4 16.1 %collective-permute-start.23 = (bf16[24,3072]{1,0:T(8,128)(2,1)S(1)}, bf16[24,3072]{1,0:T(8,128)(2,1)S(1)}, u32[]{:S(2)}, u32[]{:S(2)}) collective-permute-start(bf16[24,3072]{1,0:T(8,128)(2,1)S(1)} %fusion.56), channel_id=1, source_target_pairs={{8,4},{9,5},{10,6},{11,7},{12,0},{13,1},{14,2},{15,3},{16,12},{17,... | collective-permute-start | bytes 442376 | tf_op jit(solution)/shard_map/ppermute | solution.py:39
  237.7 14.8 %collective-permute-start.22 = (bf16[24,3072]{1,0:T(8,128)(2,1)S(1)}, bf16[24,3072]{1,0:T(8,128)(2,1)S(1)}, u32[]{:S(2)}, u32[]{:S(2)}) collective-permute-start(bf16[24,3072]{1,0:T(8,128)(2,1)S(1)} %fusion.56), channel_id=1, source_target_pairs={{8,2},{9,3},{10,0},{11,1},{12,6},{13,7},{14,4},{15,5},{16,10},{17,... | collective-permute-start | bytes 442376 | tf_op jit(solution)/shard_map/ppermute | solution.py:39
  239.0 15.8 %collective-permute-start.21 = (bf16[24,3072]{1,0:T(8,128)(2,1)S(1)}, bf16[24,3072]{1,0:T(8,128)(2,1)S(1)}, u32[]{:S(2)}, u32[]{:S(2)}) collective-permute-start(bf16[24,3072]{1,0:T(8,128)(2,1)S(1)} %fusion.56), channel_id=1, source_target_pairs={{8,0},{9,1},{10,2},{11,3},{12,4},{13,5},{14,6},{15,7},{16,8},{17,9... | collective-permute-start | bytes 442376 | tf_op jit(solution)/shard_map/ppermute | solution.py:39
  310.8 6.2 %collective-permute-start.27 = (bf16[24,3072]{1,0:T(8,128)(2,1)S(1)}, bf16[24,3072]{1,0:T(8,128)(2,1)S(1)}, u32[]{:S(2)}, u32[]{:S(2)}) collective-permute-start(bf16[24,3072]{1,0:T(8,128)(2,1)S(1)} %get-tuple-element.25), channel_id=1, source_target_pairs={{0,2},{1,3},{2,0},{3,1},{4,6},{5,7},{6,4},{7,5},{8,10},{9,11},{10,... | collective-permute-start | bytes 442376 | tf_op jit(solution)/shard_map/ppermute | solution.py:31
  311.4 10.2 %collective-permute-start.29 = (bf16[24,3072]{1,0:T(8,128)(2,1)S(1)}, bf16[24,3072]{1,0:T(8,128)(2,1)S(1)}, u32[]{:S(2)}, u32[]{:S(2)}) collective-permute-start(bf16[24,3072]{1,0:T(8,128)(2,1)S(1)} %get-tuple-element.26), channel_id=1, source_target_pairs={{0,6},{1,7},{2,4},{3,5},{4,2},{5,3},{6,0},{7,1},{8,14},{9,15},{10,... | collective-permute-start | bytes 442376 | tf_op jit(solution)/shard_map/ppermute | solution.py:31
  313.7 13.9 %collective-permute-start.28 = (bf16[24,3072]{1,0:T(8,128)(2,1)S(1)}, bf16[24,3072]{1,0:T(8,128)(2,1)S(1)}, u32[]{:S(2)}, u32[]{:S(2)}) collective-permute-start(bf16[24,3072]{1,0:T(8,128)(2,1)S(1)} %get-tuple-element.27), channel_id=1, source_target_pairs={{0,4},{1,5},{2,6},{3,7},{4,0},{5,1},{6,2},{7,3},{8,12},{9,13},{10,... | collective-permute-start | bytes 442376 | tf_op jit(solution)/shard_map/ppermute | solution.py:31
  328.4 12.2 %collective-permute-start.33 = (bf16[24,3072]{1,0:T(8,128)(2,1)}, bf16[24,3072]{1,0:T(8,128)(2,1)S(1)}, u32[]{:S(2)}, u32[]{:S(2)}) collective-permute-start(bf16[24,3072]{1,0:T(8,128)(2,1)} %fusion.52), channel_id=1, source_target_pairs={{8,6},{9,7},{10,4},{11,5},{12,2},{13,3},{14,0},{15,1},{16,14},{17,... | collective-permute-start | bytes 442376 | tf_op jit(solution)/shard_map/ppermute | solution.py:39
  329.7 17.2 %collective-permute-start.32 = (bf16[24,3072]{1,0:T(8,128)(2,1)}, bf16[24,3072]{1,0:T(8,128)(2,1)}, u32[]{:S(2)}, u32[]{:S(2)}) collective-permute-start(bf16[24,3072]{1,0:T(8,128)(2,1)} %fusion.52), channel_id=1, source_target_pairs={{8,4},{9,5},{10,6},{11,7},{12,0},{13,1},{14,2},{15,3},{16,12},{17,... | collective-permute-start | bytes 442376 | tf_op jit(solution)/shard_map/ppermute | solution.py:39
  331.0 15.9 %collective-permute-start.31 = (bf16[24,3072]{1,0:T(8,128)(2,1)}, bf16[24,3072]{1,0:T(8,128)(2,1)}, u32[]{:S(2)}, u32[]{:S(2)}) collective-permute-start(bf16[24,3072]{1,0:T(8,128)(2,1)} %fusion.52), channel_id=1, source_target_pairs={{8,2},{9,3},{10,0},{11,1},{12,6},{13,7},{14,4},{15,5},{16,10},{17,... | collective-permute-start | bytes 442376 | tf_op jit(solution)/shard_map/ppermute | solution.py:39
  332.3 16.3 %collective-permute-start.30 = (bf16[24,3072]{1,0:T(8,128)(2,1)}, bf16[24,3072]{1,0:T(8,128)(2,1)S(1)}, u32[]{:S(2)}, u32[]{:S(2)}) collective-permute-start(bf16[24,3072]{1,0:T(8,128)(2,1)} %fusion.52), channel_id=1, source_target_pairs={{8,0},{9,1},{10,2},{11,3},{12,4},{13,5},{14,6},{15,7},{16,8},{17,9... | collective-permute-start | bytes 442376 | tf_op jit(solution)/shard_map/ppermute | solution.py:39
  407.9 9.1 %collective-permute-start.35 = (bf16[96,3072]{1,0:T(8,128)(2,1)}, bf16[96,3072]{1,0:T(8,128)(2,1)S(1)}, u32[]{:S(2)}, u32[]{:S(2)}) collective-permute-start(bf16[96,3072]{1,0:T(8,128)(2,1)} %slice.256), channel_id=1, source_target_pairs={{0,1},{1,0},{2,3},{3,2},{4,5},{5,4},{6,7},{7,6},{8,9},{9,8},{10,11... | collective-permute-start | bytes 1769480 | tf_op jit(solution)/shard_map/ppermute | solution.py:28
  417.1 7.4 %collective-permute-start.36 = (bf16[24,3072]{1,0:T(8,128)(2,1)S(1)}, bf16[24,3072]{1,0:T(8,128)(2,1)S(1)}, u32[]{:S(2)}, u32[]{:S(2)}) collective-permute-start(bf16[24,3072]{1,0:T(8,128)(2,1)S(1)} %get-tuple-element.22), channel_id=1, source_target_pairs={{0,2},{1,3},{2,0},{3,1},{4,6},{5,7},{6,4},{7,5},{8,10},{9,11},{10,... | collective-permute-start | bytes 442376 | tf_op jit(solution)/shard_map/ppermute | solution.py:31
  418.7 9.1 %collective-permute-start.38 = (bf16[24,3072]{1,0:T(8,128)(2,1)S(1)}, bf16[24,3072]{1,0:T(8,128)(2,1)S(1)}, u32[]{:S(2)}, u32[]{:S(2)}) collective-permute-start(bf16[24,3072]{1,0:T(8,128)(2,1)S(1)} %get-tuple-element.23), channel_id=1, source_target_pairs={{0,6},{1,7},{2,4},{3,5},{4,2},{5,3},{6,0},{7,1},{8,14},{9,15},{10,... | collective-permute-start | bytes 442376 | tf_op jit(solution)/shard_map/ppermute | solution.py:31
  420.6 12.0 %collective-permute-start.37 = (bf16[24,3072]{1,0:T(8,128)(2,1)S(1)}, bf16[24,3072]{1,0:T(8,128)(2,1)S(1)}, u32[]{:S(2)}, u32[]{:S(2)}) collective-permute-start(bf16[24,3072]{1,0:T(8,128)(2,1)S(1)} %get-tuple-element.24), channel_id=1, source_target_pairs={{0,4},{1,5},{2,6},{3,7},{4,0},{5,1},{6,2},{7,3},{8,12},{9,13},{10,... | collective-permute-start | bytes 442376 | tf_op jit(solution)/shard_map/ppermute | solution.py:31
  (19 other events, 205.6 us)

commit v2 on v1

v2 whole, which is shorter than its diff:
```python
import functools

import jax
import jax.numpy as jnp
from jax import lax
from jax.experimental import pallas as pl
from jax.experimental.pallas import tpu as pltpu
from jax.sharding import PartitionSpec as P


EXPERTS = 4
CHUNKS = 2
ROWS_DOT = (((1,), (1,)), ((), ()))
VMEM_SPEC = pl.BlockSpec(memory_space=pltpu.VMEM)
SMEM_SPEC = pl.BlockSpec(memory_space=pltpu.SMEM)
ANY_SPEC = pl.BlockSpec(memory_space=pl.ANY)


def silu_parts(values):
    sig = jax.nn.sigmoid(values)
    return (values * sig, sig * (1.0 + values * (1.0 - sig)))


def tile_of(total, wanted):
    while total % wanted:
        wanted //= 2
    return wanted


def hidden_kernel(pieces, column, tile, depth, first, last, active, *refs):
    @pl.when(active[0] == 1)
    def _():
        hidden_body(pieces, column, tile, depth, first, last, list(refs))


def hidden_body(pieces, column, tile, depth, first, last, refs):
    parts = [refs.pop(0) for _ in range(pieces)]
    weight = refs.pop(0)
    streamed = [] if first else [refs.pop(0)]
    if last:
        streamed += [refs.pop(0) for _ in range(3)]
        gate_grad, lift_grad, slots = refs.pop(0), refs.pop(0), refs.pop(0)
    else:
        hidden = refs.pop(0)
    grads, buffer, sems = refs.pop(0), refs.pop(0), refs.pop(0)
    side, side_sems = refs if streamed else (None, None)
    block, width = parts[0].shape
    steps = weight.shape[0] // tile

    def weight_copy(i, slot):
        rows = weight.at[pl.ds(i * tile, tile), pl.ds(column, width)]
        return pltpu.make_async_copy(rows, buffer.at[slot], sems.at[slot])

    def side_copies(i, slot):
        cols = pl.ds(pl.multiple_of(i * tile, tile), tile)
        return [
            pltpu.make_async_copy(ref.at[:, cols], side.at[slot, j], side_sems.at[slot, j])
            for j, ref in enumerate(streamed)
        ]

    for i in range(min(depth - 1, steps)):
        weight_copy(i, i).start()
    for copy in side_copies(0, 0):
        copy.start()
    for j, part in enumerate(parts):
        grads[j * block : (j + 1) * block, :] = part[...]
    if last:
        slots[...] = jnp.zeros_like(slots)

    @pl.loop(0, steps)
    def _(i):
        slot, side_slot = lax.rem(i, depth), lax.rem(i, 2)

        @pl.when(i + depth - 1 < steps)
        def _():
            weight_copy(i + depth - 1, lax.rem(i + depth - 1, depth)).start()

        @pl.when(i + 1 < steps)
        def _():
            for copy in side_copies(i + 1, 1 - side_slot):
                copy.start()

        weight_copy(i, slot).wait()
        got = lax.dot_general(
            grads[...], buffer[slot], ROWS_DOT, preferred_element_type=jnp.float32
        )
        for copy in side_copies(i, side_slot):
            copy.wait()
        if not first:
            got = got + side[side_slot, 0]
        cols = pl.ds(pl.multiple_of(i * tile, tile), tile)
        if last:
            at = len(streamed) - 3
            gate_grad[:, cols] = (got * side[side_slot, at]).astype(jnp.bfloat16)
            lift_grad[:, cols] = (got * side[side_slot, at + 1]).astype(jnp.bfloat16)
            slots[...] += jnp.sum(got * side[side_slot, at + 2], axis=1, keepdims=True)
        else:
            hidden[:, cols] = got


def hidden_part(active, parts, weight, column, before, factors):
    block, width = parts[0].shape
    rows, units = block * len(parts), weight.shape[0]
    tile, depth = tile_of(units, 512), 4
    last = factors is not None
    streamed = ([] if before is None else [before]) + (list(factors) if last else [])
    if last:
        outs = (jax.ShapeDtypeStruct((rows, units), jnp.bfloat16),) * 2 + (
            jax.ShapeDtypeStruct((rows, 1), jnp.float32),
        )
    else:
        outs = (jax.ShapeDtypeStruct((rows, units), jnp.float32),)
    scratch = [
        pltpu.VMEM((rows, width), jnp.bfloat16),
        pltpu.VMEM((depth, tile, width), jnp.bfloat16),
        pltpu.SemaphoreType.DMA((depth,)),
    ]
    if streamed:
        scratch += [
            pltpu.VMEM((2, len(streamed), rows, tile), jnp.float32),
            pltpu.SemaphoreType.DMA((2, len(streamed))),
        ]
    return pl.pallas_call(
        functools.partial(
            hidden_kernel, len(parts), column, tile, depth, before is None, last
        ),
        in_specs=[SMEM_SPEC] + [VMEM_SPEC] * len(parts) + [ANY_SPEC] * (1 + len(streamed)),
        out_specs=(VMEM_SPEC,) * len(outs),
        out_shape=outs,
        scratch_shapes=scratch,
        cost_estimate=pl.CostEstimate(
            flops=2 * rows * width * units,
            bytes_accessed=2 * width * units + 4 * rows * units * len(streamed),
            transcendentals=0,
        ),
        compiler_params=pltpu.CompilerParams(vmem_limit_bytes=36 * 2**20),
    )(active, *parts, weight, *streamed)


def moved_kernel(row, tile, depth, active, *refs):
    @pl.when(active[0] == 1)
    def _():
        moved_body(row, tile, depth, *refs)


def moved_body(row, tile, depth, gate_grad, lift_grad, gate, lift, keep, send, bufs, sems):
    steps = keep.shape[1] // tile
    half = keep.shape[0]

    def copies(i, slot):
        rows = pl.ds(row + i * tile, tile)
        return [
            pltpu.make_async_copy(ref.at[rows], bufs.at[slot, j], sems.at[slot, j])
            for j, ref in enumerate((gate, lift))
        ]

    for i in range(min(depth - 1, steps)):
        for copy in copies(i, i):
            copy.start()

    @pl.loop(0, steps)
    def _(i):
        slot = lax.rem(i, depth)

        @pl.when(i + depth - 1 < steps)
        def _():
            for copy in copies(i + depth - 1, lax.rem(i + depth - 1, depth)):
                copy.start()

        first, second = copies(i, slot)
        first.wait()
        got = lax.dot_general(
            gate_grad[...], bufs[slot, 0], ROWS_DOT, preferred_element_type=jnp.float32
        )
        second.wait()
        got = got + lax.dot_general(
            lift_grad[...], bufs[slot, 1], ROWS_DOT, preferred_element_type=jnp.float32
        )
        cols = pl.ds(pl.multiple_of(i * tile, tile), tile)
        keep[:, cols] = got[:half]
        send[:, cols] = got[half:].astype(jnp.bfloat16)


def moved_part(active, gate_grad, lift_grad, gate, lift, row, width):
    rows, units = gate_grad.shape
    tile, depth = tile_of(width, 256), 3
    half = rows // 2
    return pl.pallas_call(
        functools.partial(moved_kernel, row, tile, depth),
        in_specs=[SMEM_SPEC, VMEM_SPEC, VMEM_SPEC, ANY_SPEC, ANY_SPEC],
        out_specs=(VMEM_SPEC, VMEM_SPEC),
        out_shape=(
            jax.ShapeDtypeStruct((half, width), jnp.float32),
            jax.ShapeDtypeStruct((half, width), jnp.bfloat16),
        ),
        scratch_shapes=[
            pltpu.VMEM((depth, 2, tile, units), jnp.bfloat16),
            pltpu.SemaphoreType.DMA((depth, 2)),
        ],
        cost_estimate=pl.CostEstimate(
            flops=4 * rows * width * units, bytes_accessed=4 * width * units, transcendentals=0
        ),
        compiler_params=pltpu.CompilerParams(vmem_limit_bytes=28 * 2**20),
    )(active, gate_grad, lift_grad, gate, lift)


def per_device(saved_inputs, expert_ids, combine, top_grad, w_gate, w_up, w_down):
    devices = lax.axis_size("expert")
    sections = lax.axis_size("section")
    lanes = devices // 2
    me = lax.axis_index("expert")
    my_section = lax.axis_index("section")
    my_lane, my_core = me // 2, me % 2
    own_expert = me // (devices // EXPERTS)
    gate_part, lift_part, down_part = w_gate[0], w_up[0], w_down[0]
    micro, tokens, width = saved_inputs.shape[1:]
    choose = expert_ids.shape[3]
    block = micro * tokens
    half = lanes * block
    chunk = width // CHUNKS

    def to_core(rows):
        return lax.ppermute(rows, "expert", [(i, i ^ 1) for i in range(devices)])

    def to_lane(rows, k):
        return lax.ppermute(rows, "expert", [(i, i ^ (2 * k)) for i in range(devices)])

    def to_lower_lane(rows, k):
        pairs = [
            (s * devices + i, (s - 1) * devices + (i ^ (2 * k)))
            for s in range(1, sections)
            for i in range(devices)
        ]
        return lax.ppermute(rows, ("section", "expert"), pairs)

    def gather(rows):
        mine = [rows] + [to_lane(rows, k) for k in range(1, lanes)]
        return mine + [to_core(part) for part in mine]

    def own_slots(sums):
        other = to_core(sums[half:].astype(jnp.bfloat16)).astype(jnp.float32)
        pair = sums[:half].astype(jnp.bfloat16).astype(jnp.float32) + other
        pair = pair.reshape(lanes, block)
        mine = [pair[0]] + [to_lane(pair[k], k) for k in range(1, lanes)]
        expert_of = (lane_of * 2) // (devices // EXPERTS)
        own = lax.dynamic_index_in_dim(chosen, me, 0, keepdims=False).reshape(block, choose)
        out = jnp.zeros((block, choose), jnp.float32)
        for k in range(lanes):
            out = out + jnp.where(own == expert_of[k], mine[k][:, None], 0.0)
        return out

    lane_of = my_lane ^ jnp.arange(lanes)
    core_of = my_core ^ jnp.arange(2)
    source = (lane_of[None, :] * 2 + core_of[:, None]).reshape(-1)
    chosen = jnp.moveaxis(expert_ids[0].reshape(micro, devices, tokens, choose), 1, 0)
    weight = jnp.moveaxis(combine[0].reshape(micro, devices, tokens, choose), 1, 0)
    routed = jnp.sum(
        jnp.where(chosen == own_expert, weight.astype(jnp.float32), 0.0), axis=-1
    )
    routed = jnp.take(routed, source, axis=0).reshape(-1)

    mine = gather(saved_inputs[0].reshape(block, width))
    inputs = jnp.concatenate(mine, axis=0)
    pre_gate = jnp.dot(inputs, gate_part, preferred_element_type=jnp.float32)
    pre_lift = jnp.dot(inputs, lift_part, preferred_element_type=jnp.float32)
    active, slope = silu_parts(pre_gate)
    factors = (
        routed[:, None] * pre_lift * slope,
        routed[:, None] * active,
        active * pre_lift,
    )

    top, mine = lax.optimization_barrier((top_grad.reshape(block, width), mine))
    upper = [top[:, c * chunk : (c + 1) * chunk] for c in range(CHUNKS)]
    pieces = [gather(part) for part in upper]
    pieces, _ = lax.optimization_barrier((pieces, pre_gate))
    results = [jnp.zeros((block, chunk), jnp.bfloat16) for _ in range(CHUNKS)]
    slots_all = jnp.zeros((devices * block, 1), jnp.float32)
    turns = [my_section == sections - 1 - step for step in range(sections)]
    active = [turn.astype(jnp.int32).reshape(1) for turn in turns]
    hidden = hidden_part(active[0], pieces[0], down_part, 0, None, None)[0]
    for step in range(sections):
        valid = turns[step]
        gate_grad, lift_grad, slots = hidden_part(
            active[step], pieces[1], down_part, chunk, hidden, factors
        )
        slots_all = jnp.where(valid, slots, slots_all)
        if step == sections - 1:
            slots_out = own_slots(slots_all.reshape(-1))
        next_upper, pieces = [], []
        for c in range(CHUNKS):
            keep, send = moved_part(
                active[step],
                gate_grad,
                lift_grad,
                gate_part,
                lift_part,
                c * chunk,
                chunk,
            )
            pair = keep + to_core(send).astype(jnp.float32)
            pair = pair.reshape(lanes, block, chunk)
            back = [
                to_lane(pair[k].astype(jnp.bfloat16), k) for k in range(1, lanes)
            ]
            total = upper[c].astype(jnp.float32) + pair[0]
            for part in back:
                total = total + part.astype(jnp.float32)
            result = total.astype(jnp.bfloat16)
            results[c] = jnp.where(valid, result, results[c])
            if step < sections - 1:
                arrived = [to_lower_lane(result, k) for k in range(lanes)]
                pieces.append(arrived + [to_core(part) for part in arrived])
                next_upper.append(arrived[0])
        upper = next_upper
        if step < sections - 1:
            hidden = hidden_part(
                active[step + 1], pieces[0], down_part, 0, None, None
            )[0]

    return (
        jnp.concatenate(results, axis=1).reshape(1, micro, tokens, width),
        slots_out.reshape(1, micro, tokens, choose),
    )


def solution(mesh):
    placed = (
        P("section", None, "expert", None),
        P("section", None, None, None),
        P("section", None, None, None),
        P(None, "expert", None),
        P("section", None, "expert"),
        P("section", None, "expert"),
        P("section", "expert", None),
    )
    return jax.shard_map(
        per_device,
        mesh=mesh,
        in_specs=placed,
        out_specs=(P("section", None, "expert", None), P("section", None, "expert", None)),
        check_vma=False,
    )
```

time: 441 us -> 372 us (0.84); the launches traced: 434 us -> 371 us
  matrix products: 223 us -> 22.5 us
  waiting for transfers between devices: 112 us -> 192 us
  Pallas kernels: 0 us -> 44.8 us
  starting transfers between devices: 48 us -> 88.7 us
  local copies, waits for them, and re-layouts: 32.6 us -> 15.5 us
  other arithmetic: 17.1 us -> 6.37 us
    dot_general x12 -> x0, matrix products: 195 us -> none  [the longest x4 74.2 us: per_device(): jnp.einsum('rf,df->rd', lift_grad, lift_part, preferred_element_type=jnp....]
    ppermute x12 -> x24, waiting for transfers between devices: 43.1 us -> 144 us  [to_lower_lane(): return lax.ppermute(rows, ('section', 'expert'), pairs)]
    pallas_call x0 -> x16, Pallas kernels: none -> 44.8 us  [the longest x8 25.5 us: moved_part(): pl.pallas_call(functools.partial(moved_kernel, row, tile, depth), in_spec...]
    ppermute x21 -> x36, waiting for transfers between devices: 63.2 us -> 43 us  [to_lane(): lax.ppermute(rows, 'expert', [(i, i ^ 2 * k) for i in range(devices)])]
    ppermute x21 -> x36, starting transfers between devices: 30 us -> 47.9 us  [to_lane(): lax.ppermute(rows, 'expert', [(i, i ^ 2 * k) for i in range(devices)])]
    ppermute x12 -> x24, starting transfers between devices: 15.5 us -> 31.3 us  [to_lower_lane(): return lax.ppermute(rows, ('section', 'expert'), pairs)]
    ppermute x10 -> x45, starting transfers between devices: 2.51 us -> 9.49 us  [to_core(): return lax.ppermute(rows, 'expert', [(i, i ^ 1) for i in range(devices)])]
    unnamed x39 -> x68, local copies, waits for them, and re-layouts: 17.9 us -> 11 us
  transfers between devices with their start and end apart: 43 -> 105, of which waited for: 29 -> 37; matrix products, arithmetic and copies ran while one was open for 9% -> 9% of each run, Pallas kernels for 0% -> 3%
where the time goes in v2:
time: 372 us; the launch traced here: 371 us
  waiting for transfers between devices  192 us (52%)
  starting transfers between devices  88.7 us (24%)
  Pallas kernels  44.8 us (12%)
  matrix products  22.5 us (6%)
  local copies, waits for them, and re-layouts  15.5 us (4%)
  other arithmetic  6.37 us (2%)
    ppermute x24, waiting for transfers between devices, to_lower_lane(): return lax.ppermute(rows, ('section', 'expert'), pairs)  144 us
    ppermute x36, starting transfers between devices, to_lane(): lax.ppermute(rows, 'expert', [(i, i ^ 2 * k) for i in range(devices)])  47.9 us
    ppermute x36, waiting for transfers between devices, to_lane(): lax.ppermute(rows, 'expert', [(i, i ^ 2 * k) for i in range(devices)])  43 us
    ppermute x24, starting transfers between devices, to_lower_lane(): return lax.ppermute(rows, ('section', 'expert'), pairs)  31.3 us
    pallas_call x8, Pallas kernels, moved_part(): pl.pallas_call(functools.partial(moved_kernel, row, tile, depth), in_spec...  25.5 us
    pallas_call x8, Pallas kernels, hidden_part(): pl.pallas_call(functools.partial(hidden_kernel, len(parts), column, tile,...  19.4 us
    dot_general x1, matrix products, per_device(): pre_lift = jnp.dot(inputs, lift_part, preferred_element_type=jnp.float32)  11.7 us
    unnamed x68, local copies, waits for them, and re-layouts  11 us
  transfers between devices with their start and end apart: 105, of which 37 were waited for; matrix products, arithmetic and copies ran while one was open for 9% of the time, Pallas kernels for 3%

profile of v2, /device:TPU:0, one launch (start us, length us, event | category | flops | bytes accessed | tf_op | source)
XLA Modules:
  0.0 371.4 jit_solution(4372477763116850767)
XLA Ops:
  2.2 4.7 %collective-permute-start.2 = (bf16[24,3072]{1,0:T(8,128)(2,1)S(1)}, bf16[24,3072]{1,0:T(8,128)(2,1)S(1)}, u32[]{:S(2)}, u32[]{:S(2)}) collective-permute-start(bf16[24,3072]{1,0:T(8,128)(2,1)S(1)} %reshape_squeeze.7), channel_id=1, source_target_pairs={{0,6},{1,7},{2,4},{3,5},{4,2},{5,3},{6,0},{7,1},{8,14},{9,15},{10,... | collective-permute-start | bytes 442376 | tf_op jit(solution)/shard_map/ppermute | solution.py:226
  11.8 8.1 %collective-permute-done.1 = bf16[24,3072]{1,0:T(8,128)(2,1)S(1)} collective-permute-done((bf16[24,3072]{1,0:T(8,128)(2,1)S(1)}, bf16[24,3072]{1,0:T(8,128)(2,1)S(1)}, u32[]{:S(2)}, u32[]{:S(2)}) %collective-permute-start.1) | collective-permute-done | bytes 147488 | tf_op jit(solution)/shard_map/ppermute | solution.py:226
  21.9 2.5 collective-permute-start.16
  26.3 2.5 collective-permute-start.9
  28.9 2.4 collective-permute-done.15.refs_2_
  32.0 10.8 %fusion.42 = f32[192,4096]{1,0:T(8,128)S(1)} fusion(bf16[192,3072]{1,0:T(8,128)(2,1)S(1)} %constant_dynamic-update-slice_fusion, bf16[1,3072,4096]{2,1,0:T(8,128)(2,1)} %param.11), kind=kOutput, calls=%fused_computation.94 | convolution fusion | flops 4831838208 | bytes 29491200 | tf_op jit(solution)/shard_map/dot_general | solution.py:264
  44.4 11.7 %fusion.1 = (f32[192,4096]{1,0:T(8,128)S(1)}, f32[192,4096]{1,0:T(8,128)S(1)}, f32[192,4096]{1,0:T(8,128)S(1)}) fusion(f32[192,4096]{1,0:T(8,128)S(1)} %fusion.42, f32[192]{0:T(256)S(1)} %select_n.169, bf16[192,3072]{1,0:T(8,128)(2,1)} %copy-done.27, bf16[1,3072,4096]{2,1,0:T(8,128)(2,1)} %param.12), kind=kOutput, calls=%fused_computation.13 | convolution fusion | flops 4841275392 | bytes 38929152 | tf_op jit(solution)/shard_map/dot_general | solution.py:265
  62.1 2.5 collective-permute-start.29
  66.7 2.5 collective-permute-start.24
  69.2 3.2 collective-permute-done.28
  73.9 4.0 %collective-permute-done.23 = bf16[24,1536]{1,0:T(8,128)(2,1)S(1)} collective-permute-done((bf16[24,1536]{1,0:T(8,128)(2,1)S(1)}, bf16[24,1536]{1,0:T(8,128)(2,1)S(1)}, u32[]{:S(2)}, u32[]{:S(2)}) %collective-permute-start.23) | collective-permute-done | bytes 73760 | tf_op jit(solution)/shard_map/ppermute | solution.py:226
  85.4 2.4 collective-permute-done.40.refs_3_
  93.5 2.1 collective-permute-done.33.refs_3_
  95.6 3.3 collective-permute-done.32.refs_2_
  115.4 6.7 %collective-permute-done.52 = bf16[24,1536]{1,0:T(8,128)(2,1)S(1)} collective-permute-done((bf16[24,1536]{1,0:T(8,128)(2,1)S(1)}, bf16[24,1536]{1,0:T(8,128)(2,1)S(1)}, u32[]{:S(2)}, u32[]{:S(2)}) %collective-permute-start.52) | collective-permute-done | bytes 73760 | tf_op jit(solution)/shard_map/ppermute | solution.py:226
  129.4 36.0 %collective-permute-done.57.refs_3_ = bf16[24,1536]{1,0:T(8,128)(2,1)S(1)} collective-permute-done((bf16[24,1536]{1,0:T(8,128)(2,1)}, bf16[24,1536]{1,0:T(8,128)(2,1)S(1)}, u32[]{:S(2)}, u32[]{:S(2)}) %collective-permute-start.57) | collective-permute-done | bytes 73760 | tf_op jit(solution)/shard_map/ppermute | solution.py:234
  173.1 39.3 %collective-permute-done.62.refs_1_ = bf16[24,1536]{1,0:T(8,128)(2,1)} collective-permute-done((bf16[24,1536]{1,0:T(8,128)(2,1)S(1)}, bf16[24,1536]{1,0:T(8,128)(2,1)}, u32[]{:S(2)}, u32[]{:S(2)}) %collective-permute-start.62) | collective-permute-done | bytes 73760 | tf_op jit(solution)/shard_map/ppermute | solution.py:234
  212.3 3.3 collective-permute-done.49.refs_0_
  223.9 2.2 collective-permute-start.77
  228.6 2.1 collective-permute-start.72
  231.1 7.0 %collective-permute-done.76 = bf16[24,1536]{1,0:T(8,128)(2,1)S(1)} collective-permute-done((bf16[24,1536]{1,0:T(8,128)(2,1)S(1)}, bf16[24,1536]{1,0:T(8,128)(2,1)S(1)}, u32[]{:S(2)}, u32[]{:S(2)}) %collective-permute-start.76) | collective-permute-done | bytes 73760 | tf_op jit(solution)/shard_map/ppermute | solution.py:226
  244.7 41.6 %collective-permute-done.81.refs_3_ = bf16[24,1536]{1,0:T(8,128)(2,1)S(1)} collective-permute-done((bf16[24,1536]{1,0:T(8,128)(2,1)S(1)}, bf16[24,1536]{1,0:T(8,128)(2,1)S(1)}, u32[]{:S(2)}, u32[]{:S(2)}) %collective-permute-start.81) | collective-permute-done | bytes 73760 | tf_op jit(solution)/shard_map/ppermute | solution.py:234
  287.6 2.2 collective-permute-done.80.refs_2_
  295.0 3.0 collective-permute-done.73.refs_0_
  301.6 6.8 %shard_map.98.refs_9_ = f32[192,4096]{1,0:T(8,128)S(1)} custom-call(s32[1]{0:T(128)} %bitcast.8.active, bf16[24,1536]{1,0:T(8,128)(2,1)S(1)} %collective-permute-done.73.refs_0_, bf16[24,1536]{1,0:T(8,128)(2,1)S(1)} %collective-permute-done.86.refs_1_, bf16[24,1536]{1,0:T(8,128)(2,1)S(1)} %collective-permute-done.87.refs_2_, ...), custom_call_target="tpu_custom_call" | custom-call | flops 2415919104 | bytes 12582912 | tf_op jit(solution)/shard_map/pallas_call | solution.py:123
  308.4 9.6 %shard_map.99 = (bf16[192,4096]{1,0:T(8,128)(2,1)S(1)}, bf16[192,4096]{1,0:T(8,128)(2,1)S(1)}, f32[192,1]{1,0:T(8,128)S(1)}) custom-call(s32[1]{0:T(128)} %bitcast.8.active, bf16[24,1536]{1,0:T(8,128)(2,1)S(1)} %collective-permute-done.78.refs_0_, bf16[24,1536]{1,0:T(8,128)(2,1)S(1)} %collective-permute-done.79.refs_1_, ...), custom_call_target="tpu_custom_call" | custom-call | flops 2415919104 | bytes 25165824 | tf_op jit(solution)/shard_map/pallas_call | solution.py:123
  318.3 12.6 %shard_map.101 = (f32[96,1536]{1,0:T(8,128)S(1)}, bf16[96,1536]{1,0:T(8,128)(2,1)S(1)}) custom-call(s32[1]{0:T(128)} %bitcast.8.active, bf16[192,4096]{1,0:T(8,128)(2,1)S(1)} %get-tuple-element.82.refs_0_, bf16[192,4096]{1,0:T(8,128)(2,1)S(1)} %get-tuple-element.83.refs_1_, bf16[3072,4096]{1,0:T(8,128)(2,1)} %bitcast.63, bf16[3072,4096]{1,0:T(8,128)(2,1)} %bitcast.71), custom_call_target="tpu_custom_call" | custom-call | flops 4831838208 | bytes 25165824 | tf_op jit(solution)/shard_map/pallas_call | solution.py:188
  330.9 12.6 %shard_map.100 = (f32[96,1536]{1,0:T(8,128)S(1)}, bf16[96,1536]{1,0:T(8,128)(2,1)S(1)}) custom-call(s32[1]{0:T(128)} %bitcast.8.active, bf16[192,4096]{1,0:T(8,128)(2,1)S(1)} %get-tuple-element.82.refs_0_, bf16[192,4096]{1,0:T(8,128)(2,1)S(1)} %get-tuple-element.83.refs_1_, bf16[3072,4096]{1,0:T(8,128)(2,1)} %bitcast.64, bf16[3072,4096]{1,0:T(8,128)(2,1)} %bitcast.72), custom_call_target="tpu_custom_call" | custom-call | flops 4831838208 | bytes 25165824 | tf_op jit(solution)/shard_map/pallas_call | solution.py:188
  345.9 3.3 collective-permute-start.102
  350.8 3.1 fusion.38
  357.8 2.9 collective-permute-start.94
  363.0 5.5 %collective-permute-done.99 = bf16[24,1536]{1,0:T(8,128)(2,1)S(1)} collective-permute-done((bf16[24,1536]{1,0:T(8,128)(2,1)S(1)}, bf16[24,1536]{1,0:T(8,128)(2,1)S(1)}, u32[]{:S(2)}, u32[]{:S(2)}) %collective-permute-start.99) | collective-permute-done | bytes 73760 | tf_op jit(solution)/shard_map/ppermute | solution.py:226
  (320 shorter events, 107.4 us)
Async XLA Ops:
  1.6 18.9 %collective-permute-start.3 = (bf16[24,3072]{1,0:T(8,128)(2,1)S(1)}, bf16[24,3072]{1,0:T(8,128)(2,1)S(1)}, u32[]{:S(2)}, u32[]{:S(2)}) collective-permute-start(bf16[24,3072]{1,0:T(8,128)(2,1)S(1)} %reshape_squeeze.7), channel_id=1, source_target_pairs={{0,1},{1,0},{2,3},{3,2},{4,5},{5,4},{6,7},{7,6},{8,9},{9,8},{10,11... | collective-permute-start | bytes 442376 | tf_op jit(solution)/shard_map/ppermute | solution.py:223
  6.8 13.1 %collective-permute-start.1 = (bf16[24,3072]{1,0:T(8,128)(2,1)S(1)}, bf16[24,3072]{1,0:T(8,128)(2,1)S(1)}, u32[]{:S(2)}, u32[]{:S(2)}) collective-permute-start(bf16[24,3072]{1,0:T(8,128)(2,1)S(1)} %reshape_squeeze.7), channel_id=1, source_target_pairs={{0,4},{1,5},{2,6},{3,7},{4,0},{5,1},{6,2},{7,3},{8,12},{9,13},{10,... | collective-permute-start | bytes 442376 | tf_op jit(solution)/shard_map/ppermute | solution.py:226
  6.8 13.1 %collective-permute-start = (bf16[24,3072]{1,0:T(8,128)(2,1)S(1)}, bf16[24,3072]{1,0:T(8,128)(2,1)S(1)}, u32[]{:S(2)}, u32[]{:S(2)}) collective-permute-start(bf16[24,3072]{1,0:T(8,128)(2,1)S(1)} %reshape_squeeze.7), channel_id=1, source_target_pairs={{0,2},{1,3},{2,0},{3,1},{4,6},{5,7},{6,4},{7,5},{8,10},{9,11},{10,... | collective-permute-start | bytes 442376 | tf_op jit(solution)/shard_map/ppermute | solution.py:226
  26.3 16.5 %collective-permute-start.10 = (bf16[24,1536]{1,0:T(8,128)(2,1)S(1)}, bf16[24,1536]{1,0:T(8,128)(2,1)S(1)}, u32[]{:S(2)}, u32[]{:S(2)}) collective-permute-start(bf16[24,1536]{1,0:T(8,128)(2,1)S(1)} %get-tuple-element.56.refs_0_), channel_id=1, source_target_pairs={{0,1},{1,0},{2,3},{3,2},{4,5},{5,4},{6,7},{7,6},{8,9},{9,8},{10,11... | collective-permute-start | bytes 221192 | tf_op jit(solution)/shard_map/ppermute | solution.py:223
  26.3 17.0 %collective-permute-start.9 = (bf16[24,1536]{1,0:T(8,128)(2,1)S(1)}, bf16[24,1536]{1,0:T(8,128)(2,1)S(1)}, u32[]{:S(2)}, u32[]{:S(2)}) collective-permute-start(bf16[24,1536]{1,0:T(8,128)(2,1)S(1)} %get-tuple-element.56.refs_0_), channel_id=1, source_target_pairs={{0,6},{1,7},{2,4},{3,5},{4,2},{5,3},{6,0},{7,1},{8,14},{9,15},{10,... | collective-permute-start | bytes 221192 | tf_op jit(solution)/shard_map/ppermute | solution.py:226
  28.9 14.5 %collective-permute-start.8 = (bf16[24,1536]{1,0:T(8,128)(2,1)S(1)}, bf16[24,1536]{1,0:T(8,128)(2,1)S(1)}, u32[]{:S(2)}, u32[]{:S(2)}) collective-permute-start(bf16[24,1536]{1,0:T(8,128)(2,1)S(1)} %get-tuple-element.56.refs_0_), channel_id=1, source_target_pairs={{0,4},{1,5},{2,6},{3,7},{4,0},{5,1},{6,2},{7,3},{8,12},{9,13},{10,... | collective-permute-start | bytes 221192 | tf_op jit(solution)/shard_map/ppermute | solution.py:226
  31.3 12.6 %collective-permute-start.7 = (bf16[24,1536]{1,0:T(8,128)(2,1)S(1)}, bf16[24,1536]{1,0:T(8,128)(2,1)S(1)}, u32[]{:S(2)}, u32[]{:S(2)}) collective-permute-start(bf16[24,1536]{1,0:T(8,128)(2,1)S(1)} %get-tuple-element.56.refs_0_), channel_id=1, source_target_pairs={{0,2},{1,3},{2,0},{3,1},{4,6},{5,7},{6,4},{7,5},{8,10},{9,11},{10,... | collective-permute-start | bytes 221192 | tf_op jit(solution)/shard_map/ppermute | solution.py:226
  42.8 13.3 %collective-permute-start.19 = (bf16[24,1536]{1,0:T(8,128)(2,1)S(1)}, bf16[24,1536]{1,0:T(8,128)(2,1)S(1)}, u32[]{:S(2)}, u32[]{:S(2)}) collective-permute-start(bf16[24,1536]{1,0:T(8,128)(2,1)S(1)} %collective-permute-done.15.refs_2_), channel_id=1, source_target_pairs={{0,1},{1,0},{2,3},{3,2},{4,5},{5,4},{6,7},{7,6},{8,9},{9,8},{10,11... | collective-permute-start | bytes 221192 | tf_op jit(solution)/shard_map/ppermute | solution.py:223
  43.4 12.8 %collective-permute-start.18 = (bf16[24,1536]{1,0:T(8,128)(2,1)S(1)}, bf16[24,1536]{1,0:T(8,128)(2,1)S(1)}, u32[]{:S(2)}, u32[]{:S(2)}) collective-permute-start(bf16[24,1536]{1,0:T(8,128)(2,1)S(1)} %collective-permute-done.14.refs_1_), channel_id=1, source_target_pairs={{0,1},{1,0},{2,3},{3,2},{4,5},{5,4},{6,7},{7,6},{8,9},{9,8},{10,11... | collective-permute-start | bytes 221192 | tf_op jit(solution)/shard_map/ppermute | solution.py:223
  43.4 12.7 %collective-permute-start.13 = (bf16[24,1536]{1,0:T(8,128)(2,1)S(1)}, bf16[24,1536]{1,0:T(8,128)(2,1)S(1)}, u32[]{:S(2)}, u32[]{:S(2)}) collective-permute-start(bf16[24,1536]{1,0:T(8,128)(2,1)S(1)} %collective-permute-done.9.refs_3_), channel_id=1, source_target_pairs={{0,1},{1,0},{2,3},{3,2},{4,5},{5,4},{6,7},{7,6},{8,9},{9,8},{10,11... | collective-permute-start | bytes 221192 | tf_op jit(solution)/shard_map/ppermute | solution.py:223
  43.9 12.3 %collective-permute-start.12 = (bf16[24,1536]{1,0:T(8,128)(2,1)S(1)}, bf16[24,1536]{1,0:T(8,128)(2,1)S(1)}, u32[]{:S(2)}, u32[]{:S(2)}) collective-permute-start(bf16[24,1536]{1,0:T(8,128)(2,1)S(1)} %collective-permute-done.8.refs_2_), channel_id=1, source_target_pairs={{0,1},{1,0},{2,3},{3,2},{4,5},{5,4},{6,7},{7,6},{8,9},{9,8},{10,11... | collective-permute-start | bytes 221192 | tf_op jit(solution)/shard_map/ppermute | solution.py:223
  44.0 12.2 %collective-permute-start.11 = (bf16[24,1536]{1,0:T(8,128)(2,1)S(1)}, bf16[24,1536]{1,0:T(8,128)(2,1)S(1)}, u32[]{:S(2)}, u32[]{:S(2)}) collective-permute-start(bf16[24,1536]{1,0:T(8,128)(2,1)S(1)} %collective-permute-done.7.refs_1_), channel_id=1, source_target_pairs={{0,1},{1,0},{2,3},{3,2},{4,5},{5,4},{6,7},{7,6},{8,9},{9,8},{10,11... | collective-permute-start | bytes 221192 | tf_op jit(solution)/shard_map/ppermute | solution.py:223
  111.4 14.0 %collective-permute-start.46 = (bf16[24,1536]{1,0:T(8,128)(2,1)S(1)}, bf16[24,1536]{1,0:T(8,128)(2,1)S(1)}, u32[]{:S(2)}, u32[]{:S(2)}) collective-permute-start(bf16[24,1536]{1,0:T(8,128)(2,1)S(1)} %get-tuple-element.129), channel_id=1, source_target_pairs={{0,2},{1,3},{2,0},{3,1},{4,6},{5,7},{6,4},{7,5},{8,10},{9,11},{10,... | collective-permute-start | bytes 221192 | tf_op jit(solution)/shard_map/ppermute | solution.py:226
  113.0 13.7 %collective-permute-start.48 = (bf16[24,1536]{1,0:T(8,128)(2,1)S(1)}, bf16[24,1536]{1,0:T(8,128)(2,1)S(1)}, u32[]{:S(2)}, u32[]{:S(2)}) collective-permute-start(bf16[24,1536]{1,0:T(8,128)(2,1)S(1)} %get-tuple-element.130), channel_id=1, source_target_pairs={{0,6},{1,7},{2,4},{3,5},{4,2},{5,3},{6,0},{7,1},{8,14},{9,15},{10,... | collective-permute-start | bytes 221192 | tf_op jit(solution)/shard_map/ppermute | solution.py:226
  122.8 42.6 %collective-permute-start.57 = (bf16[24,1536]{1,0:T(8,128)(2,1)}, bf16[24,1536]{1,0:T(8,128)(2,1)S(1)}, u32[]{:S(2)}, u32[]{:S(2)}) collective-permute-start(bf16[24,1536]{1,0:T(8,128)(2,1)} %fusion.21), channel_id=1, source_target_pairs={{8,6},{9,7},{10,4},{11,5},{12,2},{13,3},{14,0},{15,1},{16,14},{17,... | collective-permute-start | bytes 221192 | tf_op jit(solution)/shard_map/ppermute | solution.py:234
  124.1 43.8 %collective-permute-start.56 = (bf16[24,1536]{1,0:T(8,128)(2,1)}, bf16[24,1536]{1,0:T(8,128)(2,1)S(1)}, u32[]{:S(2)}, u32[]{:S(2)}) collective-permute-start(bf16[24,1536]{1,0:T(8,128)(2,1)} %fusion.21), channel_id=1, source_target_pairs={{8,4},{9,5},{10,6},{11,7},{12,0},{13,1},{14,2},{15,3},{16,12},{17,... | collective-permute-start | bytes 221192 | tf_op jit(solution)/shard_map/ppermute | solution.py:234
  125.4 43.8 %collective-permute-start.55 = (bf16[24,1536]{1,0:T(8,128)(2,1)}, bf16[24,1536]{1,0:T(8,128)(2,1)S(1)}, u32[]{:S(2)}, u32[]{:S(2)}) collective-permute-start(bf16[24,1536]{1,0:T(8,128)(2,1)} %fusion.21), channel_id=1, source_target_pairs={{8,2},{9,3},{10,0},{11,1},{12,6},{13,7},{14,4},{15,5},{16,10},{17,... | collective-permute-start | bytes 221192 | tf_op jit(solution)/shard_map/ppermute | solution.py:234
  126.8 44.3 %collective-permute-start.64 = (bf16[24,1536]{1,0:T(8,128)(2,1)S(1)}, bf16[24,1536]{1,0:T(8,128)(2,1)}, u32[]{:S(2)}, u32[]{:S(2)}) collective-permute-start(bf16[24,1536]{1,0:T(8,128)(2,1)S(1)} %fusion.25), channel_id=1, source_target_pairs={{8,6},{9,7},{10,4},{11,5},{12,2},{13,3},{14,0},{15,1},{16,14},{17,... | collective-permute-start | bytes 221192 | tf_op jit(solution)/shard_map/ppermute | solution.py:234
  128.1 45.0 %collective-permute-start.63 = (bf16[24,1536]{1,0:T(8,128)(2,1)S(1)}, bf16[24,1536]{1,0:T(8,128)(2,1)}, u32[]{:S(2)}, u32[]{:S(2)}) collective-permute-start(bf16[24,1536]{1,0:T(8,128)(2,1)S(1)} %fusion.25), channel_id=1, source_target_pairs={{8,4},{9,5},{10,6},{11,7},{12,0},{13,1},{14,2},{15,3},{16,12},{17,... | collective-permute-start | bytes 221192 | tf_op jit(solution)/shard_map/ppermute | solution.py:234
  165.4 46.9 %collective-permute-start.62 = (bf16[24,1536]{1,0:T(8,128)(2,1)S(1)}, bf16[24,1536]{1,0:T(8,128)(2,1)}, u32[]{:S(2)}, u32[]{:S(2)}) collective-permute-start(bf16[24,1536]{1,0:T(8,128)(2,1)S(1)} %fusion.25), channel_id=1, source_target_pairs={{8,2},{9,3},{10,0},{11,1},{12,6},{13,7},{14,4},{15,5},{16,10},{17,... | collective-permute-start | bytes 221192 | tf_op jit(solution)/shard_map/ppermute | solution.py:234
  167.9 47.7 %collective-permute-start.49 = (bf16[24,1536]{1,0:T(8,128)(2,1)S(1)}, bf16[24,1536]{1,0:T(8,128)(2,1)S(1)}, u32[]{:S(2)}, u32[]{:S(2)}) collective-permute-start(bf16[24,1536]{1,0:T(8,128)(2,1)S(1)} %fusion.25), channel_id=1, source_target_pairs={{8,0},{9,1},{10,2},{11,3},{12,4},{13,5},{14,6},{15,7},{16,8},{17,9... | collective-permute-start | bytes 221192 | tf_op jit(solution)/shard_map/ppermute | solution.py:234
  169.2 48.5 %collective-permute-start.54 = (bf16[24,1536]{1,0:T(8,128)(2,1)}, bf16[24,1536]{1,0:T(8,128)(2,1)S(1)}, u32[]{:S(2)}, u32[]{:S(2)}) collective-permute-start(bf16[24,1536]{1,0:T(8,128)(2,1)} %fusion.21), channel_id=1, source_target_pairs={{8,0},{9,1},{10,2},{11,3},{12,4},{13,5},{14,6},{15,7},{16,8},{17,9... | collective-permute-start | bytes 221192 | tf_op jit(solution)/shard_map/ppermute | solution.py:234
  171.1 46.7 %collective-permute-start.68 = (bf16[24,1536]{1,0:T(8,128)(2,1)}, bf16[24,1536]{1,0:T(8,128)(2,1)}, u32[]{:S(2)}, u32[]{:S(2)}) collective-permute-start(bf16[24,1536]{1,0:T(8,128)(2,1)} %collective-permute-done.64.refs_3_), channel_id=1, source_target_pairs={{0,1},{1,0},{2,3},{3,2},{4,5},{5,4},{6,7},{7,6},{8,9},{9,8},{10,11... | collective-permute-start | bytes 221192 | tf_op jit(solution)/shard_map/ppermute | solution.py:223
  173.1 45.2 %collective-permute-start.67 = (bf16[24,1536]{1,0:T(8,128)(2,1)}, bf16[24,1536]{1,0:T(8,128)(2,1)}, u32[]{:S(2)}, u32[]{:S(2)}) collective-permute-start(bf16[24,1536]{1,0:T(8,128)(2,1)} %collective-permute-done.63.refs_2_), channel_id=1, source_target_pairs={{0,1},{1,0},{2,3},{3,2},{4,5},{5,4},{6,7},{7,6},{8,9},{9,8},{10,11... | collective-permute-start | bytes 221192 | tf_op jit(solution)/shard_map/ppermute | solution.py:223
  227.5 13.2 %collective-permute-start.70 = (bf16[24,1536]{1,0:T(8,128)(2,1)S(1)}, bf16[24,1536]{1,0:T(8,128)(2,1)S(1)}, u32[]{:S(2)}, u32[]{:S(2)}) collective-permute-start(bf16[24,1536]{1,0:T(8,128)(2,1)S(1)} %get-tuple-element.123), channel_id=1, source_target_pairs={{0,2},{1,3},{2,0},{3,1},{4,6},{5,7},{6,4},{7,5},{8,10},{9,11},{10,... | collective-permute-start | bytes 221192 | tf_op jit(solution)/shard_map/ppermute | solution.py:226
  228.6 13.5 %collective-permute-start.72 = (bf16[24,1536]{1,0:T(8,128)(2,1)S(1)}, bf16[24,1536]{1,0:T(8,128)(2,1)S(1)}, u32[]{:S(2)}, u32[]{:S(2)}) collective-permute-start(bf16[24,1536]{1,0:T(8,128)(2,1)S(1)} %get-tuple-element.124), channel_id=1, source_target_pairs={{0,6},{1,7},{2,4},{3,5},{4,2},{5,3},{6,0},{7,1},{8,14},{9,15},{10,... | collective-permute-start | bytes 221192 | tf_op jit(solution)/shard_map/ppermute | solution.py:226
  238.1 48.2 %collective-permute-start.81 = (bf16[24,1536]{1,0:T(8,128)(2,1)S(1)}, bf16[24,1536]{1,0:T(8,128)(2,1)S(1)}, u32[]{:S(2)}, u32[]{:S(2)}) collective-permute-start(bf16[24,1536]{1,0:T(8,128)(2,1)S(1)} %fusion.13), channel_id=1, source_target_pairs={{8,6},{9,7},{10,4},{11,5},{12,2},{13,3},{14,0},{15,1},{16,14},{17,... | collective-permute-start | bytes 221192 | tf_op jit(solution)/shard_map/ppermute | solution.py:234
  239.4 50.3 %collective-permute-start.80 = (bf16[24,1536]{1,0:T(8,128)(2,1)S(1)}, bf16[24,1536]{1,0:T(8,128)(2,1)S(1)}, u32[]{:S(2)}, u32[]{:S(2)}) collective-permute-start(bf16[24,1536]{1,0:T(8,128)(2,1)S(1)} %fusion.13), channel_id=1, source_target_pairs={{8,4},{9,5},{10,6},{11,7},{12,0},{13,1},{14,2},{15,3},{16,12},{17,... | collective-permute-start | bytes 221192 | tf_op jit(solution)/shard_map/ppermute | solution.py:234
  240.7 51.0 %collective-permute-start.79 = (bf16[24,1536]{1,0:T(8,128)(2,1)S(1)}, bf16[24,1536]{1,0:T(8,128)(2,1)S(1)}, u32[]{:S(2)}, u32[]{:S(2)}) collective-permute-start(bf16[24,1536]{1,0:T(8,128)(2,1)S(1)} %fusion.13), channel_id=1, source_target_pairs={{8,2},{9,3},{10,0},{11,1},{12,6},{13,7},{14,4},{15,5},{16,10},{17,... | collective-permute-start | bytes 221192 | tf_op jit(solution)/shard_map/ppermute | solution.py:234
  242.1 51.1 %collective-permute-start.88 = (bf16[24,1536]{1,0:T(8,128)(2,1)S(1)}, bf16[24,1536]{1,0:T(8,128)(2,1)S(1)}, u32[]{:S(2)}, u32[]{:S(2)}) collective-permute-start(bf16[24,1536]{1,0:T(8,128)(2,1)S(1)} %fusion.17), channel_id=1, source_target_pairs={{8,6},{9,7},{10,4},{11,5},{12,2},{13,3},{14,0},{15,1},{16,14},{17,... | collective-permute-start | bytes 221192 | tf_op jit(solution)/shard_map/ppermute | solution.py:234
  243.4 51.1 %collective-permute-start.87 = (bf16[24,1536]{1,0:T(8,128)(2,1)S(1)}, bf16[24,1536]{1,0:T(8,128)(2,1)S(1)}, u32[]{:S(2)}, u32[]{:S(2)}) collective-permute-start(bf16[24,1536]{1,0:T(8,128)(2,1)S(1)} %fusion.17), channel_id=1, source_target_pairs={{8,4},{9,5},{10,6},{11,7},{12,0},{13,1},{14,2},{15,3},{16,12},{17,... | collective-permute-start | bytes 221192 | tf_op jit(solution)/shard_map/ppermute | solution.py:234
  344.0 13.7 %collective-permute-start.93 = (bf16[96,1536]{1,0:T(8,128)(2,1)S(1)}, bf16[96,1536]{1,0:T(8,128)(2,1)S(1)}, u32[]{:S(2)}, u32[]{:S(2)}) collective-permute-start(bf16[96,1536]{1,0:T(8,128)(2,1)S(1)} %get-tuple-element.85), channel_id=1, source_target_pairs={{0,1},{1,0},{2,3},{3,2},{4,5},{5,4},{6,7},{7,6},{8,9},{9,8},{10,11... | collective-permute-start | bytes 884744 | tf_op jit(solution)/shard_map/ppermute | solution.py:223
  (102 other events, 1048.7 us)
